TPU v7x, 128 devices: a whole 4x4x4 slice. The times are simulated.
128 devices in a mesh: seq: 32 (over z, y, core), ch: 4 (over x).
Axes of the slice: x: 4, y: 4, z: 4, core: 2. Of those that a mesh axis runs over, the one named last changes fastest.
Arguments:
- query_proj: bfloat16 [16384, 512], P('seq', 'ch'), may hold values from -6 to 6
- key_proj: bfloat16 [16384, 512], P('seq', 'ch'), may hold values from -6 to 6
- value_proj: bfloat16 [16384, 512], P('seq', 'ch'), may hold values from -6 to 6
- filter_taps: float32 [16384, 128], P('seq'), may hold values from -1.1 to 1.1, as said below
- skip_gain: float32 [512], P('ch'), may hold values from 0.3 to 3
- grad_mixer: bfloat16 [16384, 512], P('seq', 'ch'), may hold values from -6 to 6
Outputs:
- mixer_out: bfloat16 [16384, 512], P('seq', 'ch')
- grad_query: bfloat16 [16384, 512], P('seq', 'ch')
- grad_key: bfloat16 [16384, 512], P('seq', 'ch')
- grad_value: bfloat16 [16384, 512], P('seq', 'ch')
- grad_filter: float32 [16384, 128], P('seq', 'ch')
Inputs may be any that keep to these rules, and one draw needn't show every extreme that they name: `filter_taps`: real-valued filter taps.
All inputs are finite; a program needn't handle non-finite values.
Results may differ from a plain program's by a relative error of at most 0.001.
Values sent between devices are 32-bit elements; how exact they have to be, the bound alone decides.
No kernel may reach another device: no remote copies, remote signals or barrier semaphores. Data moves between devices by JAX's collectives and lax.ppermute only.
A program may use at most 64 MiB of HBM per device.

v0:
```python
import math

import jax
import jax.numpy as jnp
from jax import lax
from jax.sharding import PartitionSpec as P

HIGHEST = lax.Precision.HIGHEST


def from_partner(array, axis, distance):
    return lax.ppermute(array, axis, [(i, i ^ 1 << distance) for i in range(lax.axis_size(axis))])


def complex_mul(left_real, left_imag, right_real, right_imag):
    return (
        left_real * right_real - left_imag * right_imag,
        left_real * right_imag + left_imag * right_real,
    )


def reverse_bits(value, sections):
    result = value * 0
    for section in range(sections):
        result = result + value // 2**section % 2 * 2 ** (sections - 1 - section)
    return result


def apply_table(form, table_real, table_imag, data_real, data_imag):
    first = jnp.einsum(form, table_real, data_real, precision=HIGHEST) - jnp.einsum(
        form, table_imag, data_imag, precision=HIGHEST
    )
    second = jnp.einsum(form, table_real, data_imag, precision=HIGHEST) + jnp.einsum(
        form, table_imag, data_real, precision=HIGHEST
    )
    return (first, second)


def local_table(count, sign):
    index = jnp.arange(count, dtype=jnp.int32)
    angles = (
        sign * 2.0 * math.pi / count * (index[:, None] * index[None, :] % count).astype(jnp.float32)
    )
    return (jnp.cos(angles), jnp.sin(angles))


def seq_twiddle(local_rows, seq_total, freq_index, sign):
    index = jnp.arange(local_rows, dtype=jnp.int32)
    angles = sign * 2.0 * math.pi / seq_total * (index * freq_index).astype(jnp.float32)
    return (jnp.cos(angles)[None, :, None], jnp.sin(angles)[None, :, None])


def cross_forward(real_part, imag_part, seq_count, own_index):
    sections = seq_count.bit_length() - 1
    for section in reversed(range(sections)):
        block_span = 2 ** (section + 1)
        half_span = 2**section
        offset = own_index % block_span
        is_upper = offset >= half_span
        angle = -2.0 * math.pi / block_span * (offset - half_span).astype(jnp.float32)
        partner_real, partner_imag = from_partner((real_part, imag_part), "seq", section)
        diff_real, diff_imag = complex_mul(
            partner_real - real_part, partner_imag - imag_part, jnp.cos(angle), jnp.sin(angle)
        )
        real_part = jnp.where(is_upper, diff_real, real_part + partner_real)
        imag_part = jnp.where(is_upper, diff_imag, imag_part + partner_imag)
    return (real_part, imag_part)


def cross_inverse(real_part, imag_part, seq_count, own_index):
    sections = seq_count.bit_length() - 1
    for section in range(sections):
        block_span = 2 ** (section + 1)
        half_span = 2**section
        offset = own_index % block_span
        is_upper = offset >= half_span
        paired = jnp.where(is_upper, offset - half_span, offset)
        angle = 2.0 * math.pi / block_span * paired.astype(jnp.float32)
        conj_real = jnp.cos(angle)
        conj_imag = jnp.sin(angle)
        partner_real, partner_imag = from_partner((real_part, imag_part), "seq", section)
        turned_partner = complex_mul(partner_real, partner_imag, conj_real, conj_imag)
        turned_own = complex_mul(real_part, imag_part, conj_real, conj_imag)
        lower_real = 0.5 * (real_part + turned_partner[0])
        lower_imag = 0.5 * (imag_part + turned_partner[1])
        upper_real = 0.5 * (partner_real - turned_own[0])
        upper_imag = 0.5 * (partner_imag - turned_own[1])
        real_part = jnp.where(is_upper, upper_real, lower_real)
        imag_part = jnp.where(is_upper, upper_imag, lower_imag)
    return (real_part, imag_part)


def forward_transform(real_part, imag_part, seq_count, own_index):
    sections = seq_count.bit_length() - 1
    real_part, imag_part = cross_forward(real_part, imag_part, seq_count, own_index)
    local_rows = real_part.shape[1]
    freq_index = reverse_bits(own_index, sections)
    twist_real, twist_imag = seq_twiddle(local_rows, local_rows * seq_count, freq_index, -1.0)
    real_part, imag_part = complex_mul(real_part, imag_part, twist_real, twist_imag)
    table_real, table_imag = local_table(local_rows, -1.0)
    return apply_table("kj,ajw->akw", table_real, table_imag, real_part, imag_part)


def inverse_transform(real_part, imag_part, seq_count, own_index):
    sections = seq_count.bit_length() - 1
    local_rows = real_part.shape[1]
    table_real, table_imag = local_table(local_rows, 1.0)
    factor = 1.0 / local_rows
    real_part, imag_part = apply_table(
        "jk,akw->ajw", table_real * factor, table_imag * factor, real_part, imag_part
    )
    freq_index = reverse_bits(own_index, sections)
    twist_real, twist_imag = seq_twiddle(local_rows, local_rows * seq_count, freq_index, 1.0)
    real_part, imag_part = complex_mul(real_part, imag_part, twist_real, twist_imag)
    return cross_inverse(real_part, imag_part, seq_count, own_index)


def local(query_proj, key_proj, value_proj, filter_taps, skip_gain, grad_mixer):
    seq_count = lax.axis_size("seq")
    own_index = lax.axis_index("seq")
    local_rows, local_ch = query_proj.shape
    filters = filter_taps.shape[1]
    repeats = local_ch // filters
    seq_total = local_rows * seq_count
    query = query_proj.astype(jnp.float32)
    key_data = key_proj.astype(jnp.float32)
    value_data = value_proj.astype(jnp.float32)
    upstream = grad_mixer.astype(jnp.float32)
    mixed = key_data * value_data
    grad_in = upstream * query
    signals = jnp.concatenate([filter_taps, mixed, grad_in], axis=1)
    positions = own_index * local_rows + jnp.arange(local_rows, dtype=jnp.int32)
    theta = math.pi / seq_total * positions.astype(jnp.float32)
    cos_theta = jnp.cos(theta)[:, None]
    sin_theta = jnp.sin(theta)[:, None]
    start_real = jnp.stack([signals, signals * cos_theta])
    start_imag = jnp.stack([jnp.zeros_like(signals), -signals * sin_theta])
    spec_real, spec_imag = forward_transform(start_real, start_imag, seq_count, own_index)
    taps_real = jnp.tile(spec_real[:, :, :filters], (1, 1, repeats))
    taps_imag = jnp.tile(spec_imag[:, :, :filters], (1, 1, repeats))
    mixed_real = spec_real[:, :, filters : filters + local_ch]
    mixed_imag = spec_imag[:, :, filters : filters + local_ch]
    grads_real = spec_real[:, :, filters + local_ch :]
    grads_imag = spec_imag[:, :, filters + local_ch :]
    conv_real, conv_imag = complex_mul(taps_real, taps_imag, mixed_real, mixed_imag)
    back_real, back_imag = complex_mul(taps_real, -taps_imag, grads_real, grads_imag)
    corr_real, corr_imag = complex_mul(mixed_real, -mixed_imag, grads_real, grads_imag)
    corr_real = corr_real.reshape(2, local_rows, repeats, filters).sum(axis=2)
    corr_imag = corr_imag.reshape(2, local_rows, repeats, filters).sum(axis=2)
    scale = 1.0 / math.sqrt(seq_total)
    filt_real, filt_imag = (corr_real, corr_imag)
    out_real, out_imag = inverse_transform(
        jnp.concatenate([conv_real, back_real, filt_real], axis=2),
        jnp.concatenate([conv_imag, back_imag, filt_imag], axis=2),
        seq_count,
        own_index,
    )
    real_field = 0.5 * (out_real[0] + cos_theta * out_real[1] - sin_theta * out_imag[1])
    imag_field = 0.5 * (out_imag[0] + sin_theta * out_real[1] + cos_theta * out_imag[1])
    real_field, imag_field = (real_field, imag_field)
    conv = real_field[:, :local_ch]
    back_corr = real_field[:, local_ch : 2 * local_ch]
    filt_field = real_field[:, 2 * local_ch :]
    grad_filter = lax.psum_scatter(filt_field, "ch", scatter_dimension=1, tiled=True) * scale
    gain_row = skip_gain[None, :]
    pre = conv + gain_row * mixed
    mixer_out = (query * pre).astype(jnp.bfloat16)
    grad_query = (upstream * pre).astype(jnp.bfloat16)
    back = back_corr + gain_row * grad_in
    grad_key = (back * value_data).astype(jnp.bfloat16)
    grad_value = (back * key_data).astype(jnp.bfloat16)
    return (mixer_out, grad_query, grad_key, grad_value, grad_filter)


def solution(mesh):
    in_specs = (
        P("seq", "ch"),
        P("seq", "ch"),
        P("seq", "ch"),
        P("seq", None),
        P("ch"),
        P("seq", "ch"),
    )
    out_specs = (P("seq", "ch"), P("seq", "ch"), P("seq", "ch"), P("seq", "ch"), P("seq", "ch"))
    return jax.shard_map(local, mesh=mesh, in_specs=in_specs, out_specs=out_specs, check_vma=False)
```

profile of v0, /device:TPU:1, one launch (start us, length us, event | category | flops | bytes accessed | tf_op | source)
XLA Modules:
  0.0 710.5 jit_solution(17290512921748012059)
XLA Ops:
  20.1 32.9 %collective-permute-done = f32[2,512,384]{1,2,0:T(8,128)} collective-permute-done((f32[2,512,384]{1,2,0:T(8,128)}, f32[2,512,384]{1,2,0:T(8,128)}, u32[]{:S(2)}, u32[]{:S(2)}) %collective-permute-start) | collective-permute-done | bytes 1572896 | tf_op jit(solution)/shard_map/ppermute | solution.py:12
  53.0 33.7 %collective-permute-done.1 = f32[2,512,384]{1,2,0:T(8,128)} collective-permute-done((f32[2,512,384]{1,2,0:T(8,128)}, f32[2,512,384]{1,2,0:T(8,128)}, u32[]{:S(2)}, u32[]{:S(2)}) %collective-permute-start.1) | collective-permute-done | bytes 1572896 | tf_op jit(solution)/shard_map/ppermute | solution.py:12
  92.6 33.3 %collective-permute-done.2 = f32[2,512,384]{1,2,0:T(8,128)S(1)} collective-permute-done((f32[2,512,384]{1,2,0:T(8,128)}, f32[2,512,384]{1,2,0:T(8,128)S(1)}, u32[]{:S(2)}, u32[]{:S(2)}) %collective-permute-start.2) | collective-permute-done | bytes 1572896 | tf_op jit(solution)/shard_map/ppermute | solution.py:12
  127.0 32.6 %collective-permute-done.3 = f32[2,512,384]{1,2,0:T(8,128)} collective-permute-done((f32[2,512,384]{1,2,0:T(8,128)}, f32[2,512,384]{1,2,0:T(8,128)}, u32[]{:S(2)}, u32[]{:S(2)}) %collective-permute-start.3) | collective-permute-done | bytes 1572896 | tf_op jit(solution)/shard_map/ppermute | solution.py:12
  166.8 32.3 %collective-permute-done.4 = f32[2,512,384]{1,2,0:T(8,128)} collective-permute-done((f32[2,512,384]{1,2,0:T(8,128)S(1)}, f32[2,512,384]{1,2,0:T(8,128)}, u32[]{:S(2)}, u32[]{:S(2)}) %collective-permute-start.4) | collective-permute-done | bytes 1572896 | tf_op jit(solution)/shard_map/ppermute | solution.py:12
  199.1 33.7 %collective-permute-done.5 = f32[2,512,384]{1,2,0:T(8,128)} collective-permute-done((f32[2,512,384]{1,2,0:T(8,128)S(1)}, f32[2,512,384]{1,2,0:T(8,128)}, u32[]{:S(2)}, u32[]{:S(2)}) %collective-permute-start.5) | collective-permute-done | bytes 1572896 | tf_op jit(solution)/shard_map/ppermute | solution.py:12
  238.7 31.6 %collective-permute-done.6 = f32[2,512,384]{1,2,0:T(8,128)S(1)} collective-permute-done((f32[2,512,384]{1,2,0:T(8,128)}, f32[2,512,384]{1,2,0:T(8,128)S(1)}, u32[]{:S(2)}, u32[]{:S(2)}) %collective-permute-start.6) | collective-permute-done | bytes 1572896 | tf_op jit(solution)/shard_map/ppermute | solution.py:12
  271.5 32.7 %collective-permute-done.7 = f32[2,512,384]{1,2,0:T(8,128)} collective-permute-done((f32[2,512,384]{1,2,0:T(8,128)}, f32[2,512,384]{1,2,0:T(8,128)}, u32[]{:S(2)}, u32[]{:S(2)}) %collective-permute-start.7) | collective-permute-done | bytes 1572896 | tf_op jit(solution)/shard_map/ppermute | solution.py:12
  320.0 6.7 fusion.10
  326.7 7.2 %fusion.8 = f32[2,384,512]{2,1,0:T(8,128)S(1)} fusion(f32[2,512,384]{1,2,0:T(8,128)S(1)} %get-tuple-element.19, f32[2,512,384]{1,2,0:T(8,128)S(1)} %get-tuple-element.18, f32[512]{0:T(512)S(1)} %get-tuple-element.51, f32[512]{0:T(512)S(1)} %get-tuple-element.52), kind=kOutput, calls=%fused_computation.41 | convolution fusion | flops 2420768768 | bytes 4722688 | tf_op jit(solution)/shard_map/kj,ajw->akw/dot_general | solution.py:33
  333.9 6.6 subtract_bitcast_fusion.1
  340.5 6.8 add_bitcast_fusion.1
  354.8 6.7 fusion
  361.5 6.6 convolution_add_fusion
  368.1 7.3 %add_bitcast_fusion = (f32[2,512,384]{1,2,0:T(8,128)S(1)}, f32[2,512,384]{1,2,0:T(8,128)S(1)}) fusion(f32[2,384,512]{2,1,0:T(8,128)S(1)} %convolution_add_fusion, f32[512]{0:T(512)S(1)} %get-tuple-element.53, f32[512]{0:T(512)S(1)} %get-tuple-element.54, f32[2,384,512]{2,1,0:T(8,128)S(1)} %fusion.1, f32[2,512,128]{1,2,0:T(8,128)S(1)} %get-tuple-element.33, ...), kind=kOutput, calls=%fused_computation.12 | convolution fusion | flops 2423390208 | bytes 7868416 | tf_op jit(solution)/shard_map/jk,akw->ajw/dot_general | solution.py:30
  386.9 34.1 %collective-permute-done.12 = f32[2,512,384]{1,2,0:T(8,128)} collective-permute-done((f32[2,512,384]{1,2,0:T(8,128)S(1)}, f32[2,512,384]{1,2,0:T(8,128)}, u32[]{:S(2)}, u32[]{:S(2)}) %collective-permute-start.12) | collective-permute-done | bytes 1572896 | tf_op jit(solution)/shard_map/ppermute | solution.py:12
  421.0 33.7 %collective-permute-done.13 = f32[2,512,384]{1,2,0:T(8,128)} collective-permute-done((f32[2,512,384]{1,2,0:T(8,128)S(1)}, f32[2,512,384]{1,2,0:T(8,128)}, u32[]{:S(2)}, u32[]{:S(2)}) %collective-permute-start.13) | collective-permute-done | bytes 1572896 | tf_op jit(solution)/shard_map/ppermute | solution.py:12
  462.5 33.3 %collective-permute-done.14 = f32[2,512,384]{1,2,0:T(8,128)S(1)} collective-permute-done((f32[2,512,384]{1,2,0:T(8,128)}, f32[2,512,384]{1,2,0:T(8,128)S(1)}, u32[]{:S(2)}, u32[]{:S(2)}) %collective-permute-start.14) | collective-permute-done | bytes 1572896 | tf_op jit(solution)/shard_map/ppermute | solution.py:12
  497.0 32.6 %collective-permute-done.15 = f32[2,512,384]{1,2,0:T(8,128)} collective-permute-done((f32[2,512,384]{1,2,0:T(8,128)}, f32[2,512,384]{1,2,0:T(8,128)}, u32[]{:S(2)}, u32[]{:S(2)}) %collective-permute-start.15) | collective-permute-done | bytes 1572896 | tf_op jit(solution)/shard_map/ppermute | solution.py:12
  535.4 32.2 %collective-permute-done.16 = f32[2,512,384]{1,2,0:T(8,128)} collective-permute-done((f32[2,512,384]{1,2,0:T(8,128)S(1)}, f32[2,512,384]{1,2,0:T(8,128)}, u32[]{:S(2)}, u32[]{:S(2)}) %collective-permute-start.16) | collective-permute-done | bytes 1572896 | tf_op jit(solution)/shard_map/ppermute | solution.py:12
  567.6 33.7 %collective-permute-done.17 = f32[2,512,384]{1,2,0:T(8,128)} collective-permute-done((f32[2,512,384]{1,2,0:T(8,128)S(1)}, f32[2,512,384]{1,2,0:T(8,128)}, u32[]{:S(2)}, u32[]{:S(2)}) %collective-permute-start.17) | collective-permute-done | bytes 1572896 | tf_op jit(solution)/shard_map/ppermute | solution.py:12
  608.5 31.5 %collective-permute-done.18 = f32[2,512,384]{1,2,0:T(8,128)} collective-permute-done((f32[2,512,384]{1,2,0:T(8,128)S(1)}, f32[2,512,384]{1,2,0:T(8,128)}, u32[]{:S(2)}, u32[]{:S(2)}) %collective-permute-start.18) | collective-permute-done | bytes 1572896 | tf_op jit(solution)/shard_map/ppermute | solution.py:12
  640.0 33.7 %collective-permute-done.19 = f32[2,512,384]{1,2,0:T(8,128)} collective-permute-done((f32[2,512,384]{1,2,0:T(8,128)S(1)}, f32[2,512,384]{1,2,0:T(8,128)}, u32[]{:S(2)}, u32[]{:S(2)}) %collective-permute-start.19) | collective-permute-done | bytes 1572896 | tf_op jit(solution)/shard_map/ppermute | solution.py:12
  682.4 19.6 %reduce-scatter.2.cloned.1.call-done = f32[512,32]{0,1:T(8,128)} async-done(((f32[512,128]{0,1:T(8,128)}), f32[512,32]{0,1:T(8,128)}) %reduce-scatter.2.cloned.1.call-update) | async-done | bytes 65552 | tf_op jit(solution)/shard_map/reduce_scatter | solution.py:164
  (79 shorter events, 99.3 us)
Async XLA Ops:
  7.2 694.9 %reduce-scatter.2.cloned.1.call-start = ((), (), s32[]{:S(2)}) async-start(), calls=%async_computation.1 | async-start | bytes 327680 | tf_op jit(solution)/shard_map/reduce_scatter | solution.py:164
  14.2 38.8 %collective-permute-start = (f32[2,512,384]{1,2,0:T(8,128)}, f32[2,512,384]{1,2,0:T(8,128)}, u32[]{:S(2)}, u32[]{:S(2)}) collective-permute-start(f32[2,512,384]{1,2,0:T(8,128)} %pad_maximum_fusion), channel_id=1, source_target_pairs={{0,64},{4,68},{8,72},{12,76},{16,80},{20,84},{24,88},{28,92},{32,9... | collective-permute-start | bytes 4718600 | tf_op jit(solution)/shard_map/ppermute | solution.py:12
  19.9 66.7 %collective-permute-start.1 = (f32[2,512,384]{1,2,0:T(8,128)}, f32[2,512,384]{1,2,0:T(8,128)}, u32[]{:S(2)}, u32[]{:S(2)}) collective-permute-start(f32[2,512,384]{1,2,0:T(8,128)} %stack.13), channel_id=1, source_target_pairs={{0,64},{4,68},{8,72},{12,76},{16,80},{20,84},{24,88},{28,92},{32,9... | collective-permute-start | bytes 4718600 | tf_op jit(solution)/shard_map/ppermute | solution.py:12
  90.9 34.9 %collective-permute-start.2 = (f32[2,512,384]{1,2,0:T(8,128)}, f32[2,512,384]{1,2,0:T(8,128)S(1)}, u32[]{:S(2)}, u32[]{:S(2)}) collective-permute-start(f32[2,512,384]{1,2,0:T(8,128)} %get-tuple-element.26), channel_id=1, source_target_pairs={{0,32},{4,36},{8,40},{12,44},{16,48},{20,52},{24,56},{28,60},{32,0... | collective-permute-start | bytes 4718600 | tf_op jit(solution)/shard_map/ppermute | solution.py:12
  91.7 68.0 %collective-permute-start.3 = (f32[2,512,384]{1,2,0:T(8,128)}, f32[2,512,384]{1,2,0:T(8,128)}, u32[]{:S(2)}, u32[]{:S(2)}) collective-permute-start(f32[2,512,384]{1,2,0:T(8,128)} %get-tuple-element.27), channel_id=1, source_target_pairs={{0,32},{4,36},{8,40},{12,44},{16,48},{20,52},{24,56},{28,60},{32,0... | collective-permute-start | bytes 4718600 | tf_op jit(solution)/shard_map/ppermute | solution.py:12
  163.6 35.5 %collective-permute-start.4 = (f32[2,512,384]{1,2,0:T(8,128)S(1)}, f32[2,512,384]{1,2,0:T(8,128)}, u32[]{:S(2)}, u32[]{:S(2)}) collective-permute-start(f32[2,512,384]{1,2,0:T(8,128)S(1)} %get-tuple-element.24), channel_id=1, source_target_pairs={{0,16},{4,20},{8,24},{12,28},{16,0},{20,4},{24,8},{28,12},{32,48},... | collective-permute-start | bytes 4718600 | tf_op jit(solution)/shard_map/ppermute | solution.py:12
  166.6 66.2 %collective-permute-start.5 = (f32[2,512,384]{1,2,0:T(8,128)S(1)}, f32[2,512,384]{1,2,0:T(8,128)}, u32[]{:S(2)}, u32[]{:S(2)}) collective-permute-start(f32[2,512,384]{1,2,0:T(8,128)S(1)} %get-tuple-element.25), channel_id=1, source_target_pairs={{0,16},{4,20},{8,24},{12,28},{16,0},{20,4},{24,8},{28,12},{32,48},... | collective-permute-start | bytes 4718600 | tf_op jit(solution)/shard_map/ppermute | solution.py:12
  237.1 33.2 %collective-permute-start.6 = (f32[2,512,384]{1,2,0:T(8,128)}, f32[2,512,384]{1,2,0:T(8,128)S(1)}, u32[]{:S(2)}, u32[]{:S(2)}) collective-permute-start(f32[2,512,384]{1,2,0:T(8,128)} %get-tuple-element.22), channel_id=1, source_target_pairs={{0,8},{4,12},{8,0},{12,4},{16,24},{20,28},{24,16},{28,20},{32,40},... | collective-permute-start | bytes 4718600 | tf_op jit(solution)/shard_map/ppermute | solution.py:12
  238.4 65.7 %collective-permute-start.7 = (f32[2,512,384]{1,2,0:T(8,128)}, f32[2,512,384]{1,2,0:T(8,128)}, u32[]{:S(2)}, u32[]{:S(2)}) collective-permute-start(f32[2,512,384]{1,2,0:T(8,128)} %get-tuple-element.23), channel_id=1, source_target_pairs={{0,8},{4,12},{8,0},{12,4},{16,24},{20,28},{24,16},{28,20},{32,40},... | collective-permute-start | bytes 4718600 | tf_op jit(solution)/shard_map/ppermute | solution.py:12
  308.0 7.1 collective-permute-start.8
  311.9 5.4 collective-permute-start.9
  375.4 3.6 copy-start.4
  375.4 3.6 collective-permute-start.10
  375.9 5.4 collective-permute-start.11
  385.2 35.8 %collective-permute-start.12 = (f32[2,512,384]{1,2,0:T(8,128)S(1)}, f32[2,512,384]{1,2,0:T(8,128)}, u32[]{:S(2)}, u32[]{:S(2)}) collective-permute-start(f32[2,512,384]{1,2,0:T(8,128)S(1)} %get-tuple-element.17), channel_id=1, source_target_pairs={{0,8},{4,12},{8,0},{12,4},{16,24},{20,28},{24,16},{28,20},{32,40},... | collective-permute-start | bytes 4718600 | tf_op jit(solution)/shard_map/ppermute | solution.py:12
  386.6 68.1 %collective-permute-start.13 = (f32[2,512,384]{1,2,0:T(8,128)S(1)}, f32[2,512,384]{1,2,0:T(8,128)}, u32[]{:S(2)}, u32[]{:S(2)}) collective-permute-start(f32[2,512,384]{1,2,0:T(8,128)S(1)} %get-tuple-element.16), channel_id=1, source_target_pairs={{0,8},{4,12},{8,0},{12,4},{16,24},{20,28},{24,16},{28,20},{32,40},... | collective-permute-start | bytes 4718600 | tf_op jit(solution)/shard_map/ppermute | solution.py:12
  459.4 36.4 %collective-permute-start.14 = (f32[2,512,384]{1,2,0:T(8,128)}, f32[2,512,384]{1,2,0:T(8,128)S(1)}, u32[]{:S(2)}, u32[]{:S(2)}) collective-permute-start(f32[2,512,384]{1,2,0:T(8,128)} %get-tuple-element.15), channel_id=1, source_target_pairs={{0,16},{4,20},{8,24},{12,28},{16,0},{20,4},{24,8},{28,12},{32,48},... | collective-permute-start | bytes 4718600 | tf_op jit(solution)/shard_map/ppermute | solution.py:12
  462.3 67.3 %collective-permute-start.15 = (f32[2,512,384]{1,2,0:T(8,128)}, f32[2,512,384]{1,2,0:T(8,128)}, u32[]{:S(2)}, u32[]{:S(2)}) collective-permute-start(f32[2,512,384]{1,2,0:T(8,128)} %get-tuple-element.14), channel_id=1, source_target_pairs={{0,16},{4,20},{8,24},{12,28},{16,0},{20,4},{24,8},{28,12},{32,48},... | collective-permute-start | bytes 4718600 | tf_op jit(solution)/shard_map/ppermute | solution.py:12
  533.6 34.1 %copy-start = (f32[2,512,384]{1,2,0:T(8,128)}, f32[2,512,384]{1,2,0:T(8,128)S(1)}, u32[]{:S(2)}) copy-start(f32[2,512,384]{1,2,0:T(8,128)S(1)} %get-tuple-element.12) | copy-start | bytes 4718596
  533.6 34.1 %copy-start.1 = (f32[2,512,384]{1,2,0:T(8,128)}, f32[2,512,384]{1,2,0:T(8,128)S(1)}, u32[]{:S(2)}) copy-start(f32[2,512,384]{1,2,0:T(8,128)S(1)} %get-tuple-element.13) | copy-start | bytes 4718596
  533.6 34.1 %collective-permute-start.16 = (f32[2,512,384]{1,2,0:T(8,128)S(1)}, f32[2,512,384]{1,2,0:T(8,128)}, u32[]{:S(2)}, u32[]{:S(2)}) collective-permute-start(f32[2,512,384]{1,2,0:T(8,128)S(1)} %get-tuple-element.13), channel_id=1, source_target_pairs={{0,32},{4,36},{8,40},{12,44},{16,48},{20,52},{24,56},{28,60},{32,0... | collective-permute-start | bytes 4718600 | tf_op jit(solution)/shard_map/ppermute | solution.py:12
  533.8 67.5 %collective-permute-start.17 = (f32[2,512,384]{1,2,0:T(8,128)S(1)}, f32[2,512,384]{1,2,0:T(8,128)}, u32[]{:S(2)}, u32[]{:S(2)}) collective-permute-start(f32[2,512,384]{1,2,0:T(8,128)S(1)} %get-tuple-element.12), channel_id=1, source_target_pairs={{0,32},{4,36},{8,40},{12,44},{16,48},{20,52},{24,56},{28,60},{32,0... | collective-permute-start | bytes 4718600 | tf_op jit(solution)/shard_map/ppermute | solution.py:12
  605.3 34.7 %collective-permute-start.18 = (f32[2,512,384]{1,2,0:T(8,128)S(1)}, f32[2,512,384]{1,2,0:T(8,128)}, u32[]{:S(2)}, u32[]{:S(2)}) collective-permute-start(f32[2,512,384]{1,2,0:T(8,128)S(1)} %get-tuple-element.11), channel_id=1, source_target_pairs={{0,64},{4,68},{8,72},{12,76},{16,80},{20,84},{24,88},{28,92},{32,9... | collective-permute-start | bytes 4718600 | tf_op jit(solution)/shard_map/ppermute | solution.py:12
  607.5 66.2 %collective-permute-start.19 = (f32[2,512,384]{1,2,0:T(8,128)S(1)}, f32[2,512,384]{1,2,0:T(8,128)}, u32[]{:S(2)}, u32[]{:S(2)}) collective-permute-start(f32[2,512,384]{1,2,0:T(8,128)S(1)} %get-tuple-element.10), channel_id=1, source_target_pairs={{0,64},{4,68},{8,72},{12,76},{16,80},{20,84},{24,88},{28,92},{32,9... | collective-permute-start | bytes 4718600 | tf_op jit(solution)/shard_map/ppermute | solution.py:12
  (7 other events, 12.6 us)
Sparse Core Ops, SparseCore 0:
  679.5 22.5 reduce-scatter.1
where the time goes:
time: 718 us; the launch traced here: 711 us
  waiting for transfers between devices  557 us (78%)
  matrix products  54.4 us (8%)
  other arithmetic  45.3 us (6%)
  starting transfers between devices  24.6 us (3%)
  between operations  16.2 us (2%)
  local copies, waits for them, and re-layouts  13.1 us (2%)
    ppermute x20, waiting for transfers between devices, from_partner(): lax.ppermute(array, axis, [(i, i ^ 1 << distance) for i in range(lax.axis...  537 us
    ppermute x20, starting transfers between devices, from_partner(): lax.ppermute(array, axis, [(i, i ^ 1 << distance) for i in range(lax.axis...  24.6 us
    reduce_scatter x1, waiting for transfers between devices, local(): lax.psum_scatter(filt_field, 'ch', scatter_dimension=1, tiled=True) * scale  19.6 us
    select_n x5, other arithmetic, cross_forward(): real_part = jnp.where(is_upper, diff_real, real_part + partner_real)  19 us
    select_n x4, other arithmetic, cross_inverse(): imag_part = jnp.where(is_upper, upper_imag, lower_imag)  16.5 us
  transfers between devices with their start and end apart: 21, of which 21 were waited for; matrix products, arithmetic and copies ran while one was open for 1% of the time, Pallas kernels for 0%

commit v1 on v0

v1 whole, which is shorter than its diff:
```python
import functools
import math

import jax
import jax.numpy as jnp
import numpy as np
from jax import lax
from jax.experimental import pallas as pl
from jax.experimental.pallas import tpu as pltpu
from jax.sharding import PartitionSpec as P

FINE = 128
F32 = jnp.float32
BF16 = jnp.bfloat16


def split_table(table):
    high = table.astype(BF16)
    low = (table - high.astype(np.float64)).astype(BF16)
    return high, low


@functools.lru_cache(maxsize=None)
def tables(seq_count, pieces):
    coarse = seq_count * pieces
    total = coarse * FINE
    order = (pieces * np.arange(seq_count)[None, :] + np.arange(pieces)[:, None]).reshape(-1)
    low = np.arange(coarse) + 0.5
    fine = np.arange(FINE)
    angle = -2.0 * np.pi * low[:, None] * order[None, :] / (2 * coarse)
    first = np.concatenate([np.cos(angle), np.sin(angle)], axis=0)
    first_high, first_low = split_table(first)
    first_cat = np.concatenate([first_high, first_low, first_high], axis=1)
    last_high, last_low = split_table(first.T / total)
    turn = -2.0 * np.pi * low[:, None] * fine[None, :] / (2 * total)
    twist = np.stack([np.cos(turn), np.sin(turn)]).astype(np.float32)
    wave = -2.0 * np.pi * ((fine[:, None] * fine[None, :]) % FINE) / FINE
    re, im = np.cos(wave), np.sin(wave)
    forward = np.stack(split_table(np.block([[re, im], [-im, re]])))
    inverse = np.stack(split_table(np.block([[re, -im], [im, re]])))
    return first_cat, np.stack([last_high, last_low]), twist, forward, inverse


def dot(left, right):
    return jnp.dot(left, right, preferred_element_type=F32)


def halves(value):
    high = value.astype(BF16)
    return high, (value - high.astype(F32)).astype(BF16)


def pack_kernel(pieces, rows_per, query, key, value, grad, taps, out):
    own = lax.axis_index("ch")
    count = out.shape[0] // rows_per
    for piece in range(pieces):
        rows = pl.ds(FINE * piece, FINE)
        mixed = key[rows, :].astype(F32) * value[rows, :].astype(F32)
        grad_in = grad[rows, :].astype(F32) * query[rows, :].astype(F32)
        out[pl.ds(piece, count, stride=rows_per), :] = mixed.T
        out[pl.ds(pieces + piece, count, stride=rows_per), :] = grad_in.T
    rows = pl.ds(pl.multiple_of(own * FINE, FINE), FINE)
    out[pl.ds(2 * pieces, count, stride=rows_per), :] = taps[rows, :].T


def mix_kernel(
    seq_count, pieces, rows_in, rows_out,
    data, first, last, twist, forward, inverse,
    out, part_high, part_low, spec, back_high, back_low,
):
    groups = pieces
    coarse = seq_count * pieces
    signals = 2 * groups + 1

    def gather(start, step):
        return jnp.concatenate(
            [data[pl.ds(start + step * piece, seq_count, stride=rows_in), :] for piece in range(pieces)],
            axis=0,
        )

    def load(index):
        if index == 2 * groups:
            return gather(2 * pieces, seq_count * rows_in)
        group, kind = index % groups, index // groups
        return gather(group * seq_count * rows_in + kind * pieces, 1)

    twist_re, twist_im = twist[0], twist[1]
    for begin in range(0, signals, 2):
        members = range(begin, min(begin + 2, signals))
        high, low = halves(jnp.concatenate([load(i) for i in members], axis=1))
        mid = dot(first[...], jnp.concatenate([high, high, low], axis=0))
        for place, index in enumerate(members):
            cols = slice(FINE * place, FINE * place + FINE)
            re, im = mid[:coarse, cols], mid[coarse:, cols]
            turned_re = re * twist_re - im * twist_im
            turned_im = re * twist_im + im * twist_re
            rows = slice(coarse * index, coarse * index + coarse)
            part_high[rows, :FINE], part_low[rows, :FINE] = halves(turned_re)
            part_high[rows, FINE:], part_low[rows, FINE:] = halves(turned_im)

    spec[...] = (
        dot(part_high[...], forward[0]) + dot(part_low[...], forward[0]) + dot(part_high[...], forward[1])
    )

    def spectrum(index):
        rows = slice(coarse * index, coarse * index + coarse)
        return spec[rows, :FINE], spec[rows, FINE:]

    def keep(index, re, im):
        rows = slice(coarse * index, coarse * index + coarse)
        part_high[rows, :FINE], part_low[rows, :FINE] = halves(re)
        part_high[rows, FINE:], part_low[rows, FINE:] = halves(im)

    taps_re, taps_im = spectrum(2 * groups)
    corr_re = jnp.zeros_like(taps_re)
    corr_im = jnp.zeros_like(taps_im)
    for group in range(groups):
        mixed_re, mixed_im = spectrum(group)
        grad_re, grad_im = spectrum(groups + group)
        keep(group, taps_re * mixed_re - taps_im * mixed_im, taps_re * mixed_im + taps_im * mixed_re)
        keep(groups + group, taps_re * grad_re + taps_im * grad_im, taps_re * grad_im - taps_im * grad_re)
        corr_re += mixed_re * grad_re + mixed_im * grad_im
        corr_im += mixed_re * grad_im - mixed_im * grad_re
    keep(2 * groups, corr_re, corr_im)

    spec[...] = (
        dot(part_high[...], inverse[0]) + dot(part_low[...], inverse[0]) + dot(part_high[...], inverse[1])
    )
    for index in range(signals):
        re, im = spectrum(index)
        cols = slice(FINE * index, FINE * index + FINE)
        back_high[:coarse, cols], back_low[:coarse, cols] = halves(re * twist_re + im * twist_im)
        back_high[coarse:, cols], back_low[coarse:, cols] = halves(im * twist_re - re * twist_im)

    for index in range(signals):
        cols = slice(FINE * index, FINE * index + FINE)
        result = (
            dot(last[0], back_high[:, cols]) + dot(last[0], back_low[:, cols]) + dot(last[1], back_high[:, cols])
        )
        for piece in range(pieces):
            block = result[seq_count * piece : seq_count * piece + seq_count, :]
            if index == 2 * groups:
                for group in range(groups):
                    start = group * seq_count * rows_out + 2 * pieces + piece
                    out[pl.ds(start, seq_count, stride=rows_out), :] = block
            else:
                group, kind = index % groups, index // groups
                start = group * seq_count * rows_out + kind * pieces + piece
                out[pl.ds(start, seq_count, stride=rows_out), :] = block


def unpack_kernel(
    pieces, rows_per, scale, data, query, key, value, grad, gain,
    mixer_out, grad_query, grad_key, grad_value, grad_filter,
):
    own = lax.axis_index("ch")
    count = data.shape[0] // rows_per
    owned = grad_filter.shape[0]
    gain_row = gain[...]
    for piece in range(pieces):
        rows = pl.ds(FINE * piece, FINE)
        query_data, key_data = query[rows, :].astype(F32), key[rows, :].astype(F32)
        value_data, upstream = value[rows, :].astype(F32), grad[rows, :].astype(F32)
        conv = data[pl.ds(piece, count, stride=rows_per), :].T
        pre = conv + gain_row * (key_data * value_data)
        mixer_out[rows, :] = (query_data * pre).astype(BF16)
        grad_query[rows, :] = (upstream * pre).astype(BF16)
        corr = data[pl.ds(pieces + piece, count, stride=rows_per), :].T
        back = corr + gain_row * (upstream * query_data)
        grad_key[rows, :] = (back * value_data).astype(BF16)
        grad_value[rows, :] = (back * key_data).astype(BF16)
        start = own * (owned * rows_per) + 2 * pieces + piece
        grad_filter[:, rows] = data[pl.ds(start, owned, stride=rows_per), :] * scale


def local(query_proj, key_proj, value_proj, filter_taps, skip_gain, grad_mixer):
    seq_count = lax.axis_size("seq")
    ch_count = lax.axis_size("ch")
    devices = seq_count * ch_count
    local_rows, local_ch = query_proj.shape
    pieces = local_rows // FINE
    groups = ch_count
    assert devices == local_ch and pieces == groups
    rows_in = 2 * pieces + 1
    rows_out = 3 * pieces
    seq_total = local_rows * seq_count
    coarse = seq_count * pieces
    signals = 2 * groups + 1

    packed = pl.pallas_call(
        functools.partial(pack_kernel, pieces, rows_in),
        out_shape=jax.ShapeDtypeStruct((devices * rows_in, FINE), F32),
        compiler_params=pltpu.CompilerParams(vmem_limit_bytes=8 << 20),
        name="pack",
    )(query_proj, key_proj, value_proj, grad_mixer, filter_taps)

    def exchange(array, rows):
        array = array.reshape(devices, rows, 1, FINE)
        array = lax.all_to_all(array, ("ch", "seq"), 0, 0, tiled=True)
        return array.reshape(devices * rows, FINE)

    gathered = exchange(packed, rows_in)
    constants = [jnp.asarray(table) for table in tables(seq_count, pieces)]
    mixed = pl.pallas_call(
        functools.partial(mix_kernel, seq_count, pieces, rows_in, rows_out),
        out_shape=jax.ShapeDtypeStruct((devices * rows_out, FINE), F32),
        scratch_shapes=[
            pltpu.VMEM((signals * coarse, 2 * FINE), BF16),
            pltpu.VMEM((signals * coarse, 2 * FINE), BF16),
            pltpu.VMEM((signals * coarse, 2 * FINE), F32),
            pltpu.VMEM((2 * coarse, signals * FINE), BF16),
            pltpu.VMEM((2 * coarse, signals * FINE), BF16),
        ],
        compiler_params=pltpu.CompilerParams(vmem_limit_bytes=24 << 20),
        name="mix",
    )(gathered, *constants)
    returned = exchange(mixed, rows_out)

    out_bf16 = jax.ShapeDtypeStruct((local_rows, local_ch), BF16)
    *results, grad_filter = pl.pallas_call(
        functools.partial(unpack_kernel, pieces, rows_out, 1.0 / math.sqrt(seq_total)),
        out_shape=(
            out_bf16, out_bf16, out_bf16, out_bf16,
            jax.ShapeDtypeStruct((local_ch // ch_count, local_rows), F32),
        ),
        compiler_params=pltpu.CompilerParams(vmem_limit_bytes=8 << 20),
        name="unpack",
    )(returned, query_proj, key_proj, value_proj, grad_mixer, skip_gain[None, :])
    return (*results, grad_filter.T)


def solution(mesh):
    in_specs = (
        P("seq", "ch"),
        P("seq", "ch"),
        P("seq", "ch"),
        P("seq", None),
        P("ch"),
        P("seq", "ch"),
    )
    out_specs = (P("seq", "ch"), P("seq", "ch"), P("seq", "ch"), P("seq", "ch"), P("seq", "ch"))
    return jax.shard_map(local, mesh=mesh, in_specs=in_specs, out_specs=out_specs, check_vma=False)
```

time: 718 us -> 56.9 us (0.08)
  waiting for transfers between devices: 557 us -> 0 us
  matrix products: 54.4 us -> 0 us
  blocking collectives: 0 us -> 46.3 us
  other arithmetic: 45.3 us -> 0 us
  starting transfers between devices: 24.6 us -> 0 us
  between operations: 16.2 us -> 0.76 us
  local copies, waits for them, and re-layouts: 13.1 us -> 5.25 us
    ppermute x20 -> x0, waiting for transfers between devices: 537 us -> none  [from_partner(): lax.ppermute(array, axis, [(i, i ^ 1 << distance) for i in range(lax.axis...]
    dot_general x8 -> x0, matrix products: 54.4 us -> none  [the longest x2 14 us: apply_table(): jnp.einsum(form, table_imag, data_imag, precision=HIGHEST)]
    all_to_all x0 -> x2, blocking collectives: none -> 46.3 us  [exchange(): array = lax.all_to_all(array, ('ch', 'seq'), 0, 0, tiled=True)]
    select_n x10 -> x0, other arithmetic: 38.2 us -> none  [the longest x5 19 us: cross_forward(): real_part = jnp.where(is_upper, diff_real, real_part + partner_real)]
    ppermute x20 -> x0, starting transfers between devices: 24.6 us -> none  [from_partner(): lax.ppermute(array, axis, [(i, i ^ 1 << distance) for i in range(lax.axis...]
    reduce_scatter x1 -> x0, waiting for transfers between devices: 19.6 us -> none  [local(): lax.psum_scatter(filt_field, 'ch', scatter_dimension=1, tiled=True) * scale]
  transfers between devices with their start and end apart: 21 -> 0, of which waited for: 21 -> 0; matrix products, arithmetic and copies ran while one was open for 1% -> 0% of each run, Pallas kernels for 0% -> 0%
where the time goes in v1:
time: 56.9 us; the launch traced here: 56.6 us
  blocking collectives  46.3 us (81%)
  local copies, waits for them, and re-layouts  5.25 us (9%)
  Pallas kernels  4.34 us (8%)
  between operations  0.76 us (1%)
    all_to_all x2, blocking collectives, exchange(): array = lax.all_to_all(array, ('ch', 'seq'), 0, 0, tiled=True)  46.3 us
    unnamed x30, local copies, waits for them, and re-layouts  5.25 us
    pallas_call x1, Pallas kernels, local(): pl.pallas_call(functools.partial(mix_kernel, seq_count, pieces, rows_in,...  3.08 us

profile of v1, /device:TPU:1, one launch (start us, length us, event | category | flops | bytes accessed | tf_op | source)
XLA Modules:
  0.0 56.6 jit_solution(8809081279812399554)
XLA Ops:
  0.6 0.0 copy-start
  0.6 0.9 %copy-done = bf16[512,128]{1,0:T(8,128)(2,1)S(1)} copy-done((bf16[512,128]{1,0:T(8,128)(2,1)S(1)}, bf16[512,128]{1,0:T(8,128)(2,1)}, u32[]{:S(2)}) %copy-start) | copy-done | bytes 131096
  1.5 0.9 %copy-done.2 = bf16[512,128]{1,0:T(8,128)(2,1)S(1)} copy-done((bf16[512,128]{1,0:T(8,128)(2,1)S(1)}, bf16[512,128]{1,0:T(8,128)(2,1)}, u32[]{:S(2)}) %copy-start.2) | copy-done | bytes 131096
  2.4 0.9 %copy-done.4 = bf16[512,128]{1,0:T(8,128)(2,1)S(1)} copy-done((bf16[512,128]{1,0:T(8,128)(2,1)S(1)}, bf16[512,128]{1,0:T(8,128)(2,1)}, u32[]{:S(2)}) %copy-start.4) | copy-done | bytes 131096
  3.4 0.9 %copy-done.6 = bf16[512,128]{1,0:T(8,128)(2,1)S(1)} copy-done((bf16[512,128]{1,0:T(8,128)(2,1)S(1)}, bf16[512,128]{1,0:T(8,128)(2,1)}, u32[]{:S(2)}) %copy-start.6) | copy-done | bytes 131096
  4.3 0.9 %copy-done.10 = f32[512,128]{1,0:T(8,128)S(1)} copy-done((f32[512,128]{1,0:T(8,128)S(1)}, f32[512,128]{1,0:T(8,128)}, u32[]{:S(2)}) %copy-start.10) | copy-done | bytes 262168
  5.2 0.2 pack.1
  5.4 0.0 copy-start.8
  5.4 0.0 copy-start.9
  5.5 0.0 copy-start.11
  5.5 0.0 copy-start.12
  5.5 0.0 copy-start.13
  5.5 25.5 %all_to_all.10 = f32[128,9,1,128]{3,2,1,0:T(1,128)S(1)} all-to-all(f32[128,9,1,128]{3,2,1,0:T(1,128)S(1)} %bitcast.9), channel_id=1, replica_groups=mesh['seq'=32,'ch'=4] {'ch','seq'}, dimensions={0} | all-to-all | bytes 1179648 | tf_op jit(solution)/shard_map/all_to_all | solution.py:199
  31.0 0.0 copy-done.12
  31.0 0.0 copy-done.13
  31.0 3.1 %mix.1 = f32[1536,128]{1,0:T(8,128)S(1)} custom-call(f32[1152,128]{1,0:T(8,128)S(1)} %bitcast.8, bf16[256,384]{1,0:T(8,128)(2,1)S(1)} %copy-done.11, bf16[2,128,256]{2,1,0:T(8,128)(2,1)S(1)} %copy-done.13, f32[2,128,128]{2,1,0:T(8,128)S(1)} %copy-done.12, bf16[2,256,256]{2,1,0:T(8,128)(2,1)S(1)} %copy-done.9, bf16[2,256,256]{2,1,0:T(8,128)(2,1)S(1)} %copy-done.8), custom_call_target="tpu_custom_call" | custom-call | tf_op jit(solution)/shard_map/mix/pallas_call | solution.py:204
  34.1 0.0 copy-start.1
  34.1 0.0 copy-start.3
  34.1 0.0 copy-start.5
  34.1 0.0 copy-start.7
  34.2 20.8 %all_to_all.11 = f32[128,12,1,128]{3,2,1,0:T(1,128)S(1)} all-to-all(f32[128,12,1,128]{3,2,1,0:T(1,128)S(1)} %bitcast.7), channel_id=1, replica_groups=mesh['seq'=32,'ch'=4] {'ch','seq'}, dimensions={0} | all-to-all | bytes 1572864 | tf_op jit(solution)/shard_map/all_to_all | solution.py:199
  54.9 0.0 copy-done.5
  54.9 0.6 %copy-done.14 = f32[128]{0:T(128)S(1)} copy-done((f32[128]{0:T(128)S(1)}, f32[128]{0:T(128)}, u32[]{:S(2)}) %copy-start.14) | copy-done | bytes 536
  55.6 1.0 %unpack.1 = (bf16[512,128]{1,0:T(8,128)(2,1)}, bf16[512,128]{1,0:T(8,128)(2,1)}, bf16[512,128]{1,0:T(8,128)(2,1)}, bf16[512,128]{1,0:T(8,128)(2,1)}, f32[32,512]{1,0:T(8,128)}) custom-call(f32[1536,128]{1,0:T(8,128)S(1)} %bitcast.6, bf16[512,128]{1,0:T(8,128)(2,1)S(1)} %copy-done.1, bf16[512,128]{1,0:T(8,128)(2,1)S(1)} %copy-done.3, ...), custom_call_target="tpu_custom_call" | custom-call | tf_op jit(solution)/shard_map/unpack/pallas_call | solution.py:220
  (11 shorter events, 0.0 us)
Async XLA Ops:
  0.6 0.9 %copy-start = (bf16[512,128]{1,0:T(8,128)(2,1)S(1)}, bf16[512,128]{1,0:T(8,128)(2,1)}, u32[]{:S(2)}) copy-start(bf16[512,128]{1,0:T(8,128)(2,1)} %query.3) | copy-start | bytes 393220
  1.5 0.9 %copy-start.2 = (bf16[512,128]{1,0:T(8,128)(2,1)S(1)}, bf16[512,128]{1,0:T(8,128)(2,1)}, u32[]{:S(2)}) copy-start(bf16[512,128]{1,0:T(8,128)(2,1)} %key.3) | copy-start | bytes 393220
  2.4 0.9 %copy-start.4 = (bf16[512,128]{1,0:T(8,128)(2,1)S(1)}, bf16[512,128]{1,0:T(8,128)(2,1)}, u32[]{:S(2)}) copy-start(bf16[512,128]{1,0:T(8,128)(2,1)} %value.3) | copy-start | bytes 393220
  3.3 0.9 %copy-start.6 = (bf16[512,128]{1,0:T(8,128)(2,1)S(1)}, bf16[512,128]{1,0:T(8,128)(2,1)}, u32[]{:S(2)}) copy-start(bf16[512,128]{1,0:T(8,128)(2,1)} %grad.3) | copy-start | bytes 393220
  4.3 0.9 %copy-start.10 = (f32[512,128]{1,0:T(8,128)S(1)}, f32[512,128]{1,0:T(8,128)}, u32[]{:S(2)}) copy-start(f32[512,128]{1,0:T(8,128)} %taps.1) | copy-start | bytes 786436
  5.4 25.6 %copy-start.8 = (bf16[2,256,256]{2,1,0:T(8,128)(2,1)S(1)}, bf16[2,256,256]{2,1,0:T(8,128)(2,1)}, u32[]{:S(2)}) copy-start(bf16[2,256,256]{2,1,0:T(8,128)(2,1)} %constant.14.clone.inverse) | copy-start | bytes 786436
  5.4 25.5 %copy-start.9 = (bf16[2,256,256]{2,1,0:T(8,128)(2,1)S(1)}, bf16[2,256,256]{2,1,0:T(8,128)(2,1)}, u32[]{:S(2)}) copy-start(bf16[2,256,256]{2,1,0:T(8,128)(2,1)} %constant.13.clone.forward) | copy-start | bytes 786436
  5.5 25.5 %copy-start.11 = (bf16[256,384]{1,0:T(8,128)(2,1)S(1)}, bf16[256,384]{1,0:T(8,128)(2,1)}, u32[]{:S(2)}) copy-start(bf16[256,384]{1,0:T(8,128)(2,1)} %constant.10.clone.first) | copy-start | bytes 589828
  5.5 25.5 %copy-start.12 = (f32[2,128,128]{2,1,0:T(8,128)S(1)}, f32[2,128,128]{2,1,0:T(8,128)}, u32[]{:S(2)}) copy-start(f32[2,128,128]{2,1,0:T(8,128)} %constant.12.clone.twist) | copy-start | bytes 393220
  5.5 25.5 %copy-start.13 = (bf16[2,128,256]{2,1,0:T(8,128)(2,1)S(1)}, bf16[2,128,256]{2,1,0:T(8,128)(2,1)}, u32[]{:S(2)}) copy-start(bf16[2,128,256]{2,1,0:T(8,128)(2,1)} %constant.11.clone.last) | copy-start | bytes 393220
  34.1 20.8 %copy-start.1 = (bf16[512,128]{1,0:T(8,128)(2,1)S(1)}, bf16[512,128]{1,0:T(8,128)(2,1)}, u32[]{:S(2)}) copy-start(bf16[512,128]{1,0:T(8,128)(2,1)} %query.3) | copy-start | bytes 393220
  34.1 20.8 %copy-start.3 = (bf16[512,128]{1,0:T(8,128)(2,1)S(1)}, bf16[512,128]{1,0:T(8,128)(2,1)}, u32[]{:S(2)}) copy-start(bf16[512,128]{1,0:T(8,128)(2,1)} %key.3) | copy-start | bytes 393220
  34.1 20.8 %copy-start.5 = (bf16[512,128]{1,0:T(8,128)(2,1)S(1)}, bf16[512,128]{1,0:T(8,128)(2,1)}, u32[]{:S(2)}) copy-start(bf16[512,128]{1,0:T(8,128)(2,1)} %value.3) | copy-start | bytes 393220
  34.1 20.8 %copy-start.7 = (bf16[512,128]{1,0:T(8,128)(2,1)S(1)}, bf16[512,128]{1,0:T(8,128)(2,1)}, u32[]{:S(2)}) copy-start(bf16[512,128]{1,0:T(8,128)(2,1)} %grad.3) | copy-start | bytes 393220
  54.9 0.7 %copy-start.14 = (f32[128]{0:T(128)S(1)}, f32[128]{0:T(128)}, u32[]{:S(2)}) copy-start(f32[128]{0:T(128)} %param.15) | copy-start | bytes 1540

commit v2 on v1

--- a/solution.py
+++ b/solution.py
@@ -50,17 +50,34 @@
     return high, (value - high.astype(F32)).astype(BF16)
 
 
-def pack_kernel(pieces, rows_per, query, key, value, grad, taps, out):
+def pack_kernel(pieces, rows_per, query, key, value, grad, taps, gain, out, gain_out, *scratch):
+    query_in, key_in, value_in, grad_in, taps_in, sems = scratch
     own = lax.axis_index("ch")
     count = out.shape[0] // rows_per
-    for piece in range(pieces):
-        rows = pl.ds(FINE * piece, FINE)
-        mixed = key[rows, :].astype(F32) * value[rows, :].astype(F32)
-        grad_in = grad[rows, :].astype(F32) * query[rows, :].astype(F32)
+    rows = pl.ds(pl.multiple_of(own * FINE, FINE), FINE)
+    taps_copy = pltpu.make_async_copy(taps.at[rows, :], taps_in, sems.at[4])
+    gain_copy = pltpu.make_async_copy(gain, gain_out, sems.at[5])
+    pairs = ((key, key_in), (value, value_in), (grad, grad_in), (query, query_in))
+    copies = [pltpu.make_async_copy(src, dst, sems.at[i]) for i, (src, dst) in enumerate(pairs)]
+    taps_copy.start()
+    for copy in copies:
+        copy.start()
+    gain_copy.start()
+    taps_copy.wait()
+    out[pl.ds(2 * pieces, count, stride=rows_per), :] = taps_in[...].T
+    copies[0].wait()
+    copies[1].wait()
+    for piece in range(pieces):
+        rows = pl.ds(FINE * piece, FINE)
+        mixed = key_in[rows, :].astype(F32) * value_in[rows, :].astype(F32)
         out[pl.ds(piece, count, stride=rows_per), :] = mixed.T
-        out[pl.ds(pieces + piece, count, stride=rows_per), :] = grad_in.T
-    rows = pl.ds(pl.multiple_of(own * FINE, FINE), FINE)
-    out[pl.ds(2 * pieces, count, stride=rows_per), :] = taps[rows, :].T
+    copies[2].wait()
+    copies[3].wait()
+    for piece in range(pieces):
+        rows = pl.ds(FINE * piece, FINE)
+        grads = grad_in[rows, :].astype(F32) * query_in[rows, :].astype(F32)
+        out[pl.ds(pieces + piece, count, stride=rows_per), :] = grads.T
+    gain_copy.wait()
 
 
 def mix_kernel(
@@ -151,26 +168,45 @@
 
 def unpack_kernel(
     pieces, rows_per, scale, data, query, key, value, grad, gain,
-    mixer_out, grad_query, grad_key, grad_value, grad_filter,
+    mixer_out, grad_query, grad_key, grad_value, grad_filter, *scratch,
 ):
+    holds, filter_hold, sems = scratch[:4], scratch[4], scratch[5]
     own = lax.axis_index("ch")
     count = data.shape[0] // rows_per
     owned = grad_filter.shape[0]
     gain_row = gain[...]
+    copies = []
+
+    def send(index, piece, target):
+        rows = pl.ds(FINE * piece, FINE)
+        copy = pltpu.make_async_copy(holds[index].at[rows, :], target.at[rows, :], sems.at[index, piece])
+        copy.start()
+        copies.append(copy)
+
+    for piece in range(pieces):
+        start = own * (owned * rows_per) + 2 * pieces + piece
+        filter_hold[:, FINE * piece : FINE * piece + FINE] = data[pl.ds(start, owned, stride=rows_per), :] * scale
+    filter_copy = pltpu.make_async_copy(filter_hold, grad_filter, sems.at[4, 0])
+    filter_copy.start()
     for piece in range(pieces):
         rows = pl.ds(FINE * piece, FINE)
         query_data, key_data = query[rows, :].astype(F32), key[rows, :].astype(F32)
         value_data, upstream = value[rows, :].astype(F32), grad[rows, :].astype(F32)
         conv = data[pl.ds(piece, count, stride=rows_per), :].T
         pre = conv + gain_row * (key_data * value_data)
-        mixer_out[rows, :] = (query_data * pre).astype(BF16)
-        grad_query[rows, :] = (upstream * pre).astype(BF16)
+        holds[0][rows, :] = (query_data * pre).astype(BF16)
+        send(0, piece, mixer_out)
+        holds[1][rows, :] = (upstream * pre).astype(BF16)
+        send(1, piece, grad_query)
         corr = data[pl.ds(pieces + piece, count, stride=rows_per), :].T
         back = corr + gain_row * (upstream * query_data)
-        grad_key[rows, :] = (back * value_data).astype(BF16)
-        grad_value[rows, :] = (back * key_data).astype(BF16)
-        start = own * (owned * rows_per) + 2 * pieces + piece
-        grad_filter[:, rows] = data[pl.ds(start, owned, stride=rows_per), :] * scale
+        holds[2][rows, :] = (back * value_data).astype(BF16)
+        send(2, piece, grad_key)
+        holds[3][rows, :] = (back * key_data).astype(BF16)
+        send(3, piece, grad_value)
+    filter_copy.wait()
+    for copy in copies:
+        copy.wait()
 
 
 def local(query_proj, key_proj, value_proj, filter_taps, skip_gain, grad_mixer):
@@ -187,12 +223,21 @@
     coarse = seq_count * pieces
     signals = 2 * groups + 1
 
-    packed = pl.pallas_call(
+    hbm = pl.BlockSpec(memory_space=pltpu.HBM)
+    vmem = pl.BlockSpec(memory_space=pltpu.VMEM)
+    half = pltpu.VMEM((local_rows, local_ch), BF16)
+    packed, gain_row = pl.pallas_call(
         functools.partial(pack_kernel, pieces, rows_in),
-        out_shape=jax.ShapeDtypeStruct((devices * rows_in, FINE), F32),
+        out_shape=(
+            jax.ShapeDtypeStruct((devices * rows_in, FINE), F32),
+            jax.ShapeDtypeStruct((1, local_ch), F32),
+        ),
+        in_specs=[hbm] * 6,
+        out_specs=(vmem, vmem),
+        scratch_shapes=[half] * 4 + [pltpu.VMEM((FINE, local_ch), F32), pltpu.SemaphoreType.DMA((6,))],
         compiler_params=pltpu.CompilerParams(vmem_limit_bytes=8 << 20),
         name="pack",
-    )(query_proj, key_proj, value_proj, grad_mixer, filter_taps)
+    )(*[pltpu.with_memory_space_constraint(x, pltpu.HBM) for x in (query_proj, key_proj, value_proj, grad_mixer, filter_taps, skip_gain[None, :])])
 
     def exchange(array, rows):
         array = array.reshape(devices, rows, 1, FINE)
@@ -223,9 +268,13 @@
             out_bf16, out_bf16, out_bf16, out_bf16,
             jax.ShapeDtypeStruct((local_ch // ch_count, local_rows), F32),
         ),
+        in_specs=[vmem] * 6,
+        out_specs=(hbm,) * 5,
+        scratch_shapes=[half] * 4
+        + [pltpu.VMEM((local_ch // ch_count, local_rows), F32), pltpu.SemaphoreType.DMA((5, pieces))],
         compiler_params=pltpu.CompilerParams(vmem_limit_bytes=8 << 20),
         name="unpack",
-    )(returned, query_proj, key_proj, value_proj, grad_mixer, skip_gain[None, :])
+    )(returned, query_proj, key_proj, value_proj, grad_mixer, gain_row)
     return (*results, grad_filter.T)
 
 

time: 56.9 us -> 52.7 us (0.926)
  local copies, waits for them, and re-layouts: 5.25 us -> 0.06 us
  Pallas kernels: 4.34 us -> 5.49 us
    unnamed x30 -> x18, local copies, waits for them, and re-layouts: 5.25 us -> 0.06 us
    pallas_call x1, Pallas kernels: 0.23 us -> 1.35 us  [local(): pl.pallas_call(functools.partial(pack_kernel, pieces, rows_in), out_shape...]
where the time goes in v2:
time: 52.7 us; the launch traced here: 52.5 us
  blocking collectives  46.2 us (88%)
  Pallas kernels  5.49 us (10%)
  between operations  0.75 us (1%)
    all_to_all x2, blocking collectives, exchange(): array = lax.all_to_all(array, ('ch', 'seq'), 0, 0, tiled=True)  46.2 us
    pallas_call x1, Pallas kernels, local(): pl.pallas_call(functools.partial(mix_kernel, seq_count, pieces, rows_in,...  3.08 us
    pallas_call x1, Pallas kernels, local(): pl.pallas_call(functools.partial(pack_kernel, pieces, rows_in), out_shape...  1.35 us
    pallas_call x1, Pallas kernels, local(): pl.pallas_call(functools.partial(unpack_kernel, pieces, rows_out, 1.0 / m...  1.06 us

profile of v2, /device:TPU:1, one launch (start us, length us, event | category | flops | bytes accessed | tf_op | source)
XLA Modules:
  0.0 52.5 jit_solution(4669745746096536475)
XLA Ops:
  0.6 1.3 %pack.1 = (f32[1152,128]{1,0:T(8,128)S(1)}, f32[1,128]{1,0:T(1,128)S(1)}) custom-call(bf16[512,128]{1,0:T(8,128)(2,1)} %query.3, bf16[512,128]{1,0:T(8,128)(2,1)} %key.3, bf16[512,128]{1,0:T(8,128)(2,1)} %value.3, bf16[512,128]{1,0:T(8,128)(2,1)} %grad.3, f32[512,128]{1,0:T(8,128)} %taps.1, f32[1,128]{1,0:T(1,128)} %bitcast.10), custom_call_target="tpu_custom_call" | custom-call | tf_op jit(solution)/shard_map/pack/pallas_call | solution.py:229
  2.0 0.0 copy-start.4
  2.0 0.0 copy-start.5
  2.0 0.0 copy-start.6
  2.0 0.0 copy-start.7
  2.0 0.0 copy-start.8
  2.0 25.5 %all_to_all.10 = f32[128,9,1,128]{3,2,1,0:T(1,128)S(1)} all-to-all(f32[128,9,1,128]{3,2,1,0:T(1,128)S(1)} %bitcast.9), channel_id=1, replica_groups=mesh['seq'=32,'ch'=4] {'ch','seq'}, dimensions={0} | all-to-all | bytes 1179648 | tf_op jit(solution)/shard_map/all_to_all | solution.py:244
  27.5 0.0 copy-done.4
  27.5 0.0 copy-done.5
  27.5 0.0 copy-done.6
  27.6 0.0 copy-done.7
  27.6 0.0 copy-done.8
  27.6 3.1 %mix.1 = f32[1536,128]{1,0:T(8,128)S(1)} custom-call(f32[1152,128]{1,0:T(8,128)S(1)} %bitcast.8, bf16[256,384]{1,0:T(8,128)(2,1)S(1)} %copy-done.6, bf16[2,128,256]{2,1,0:T(8,128)(2,1)S(1)} %copy-done.8, f32[2,128,128]{2,1,0:T(8,128)S(1)} %copy-done.7, bf16[2,256,256]{2,1,0:T(8,128)(2,1)S(1)} %copy-done.5, bf16[2,256,256]{2,1,0:T(8,128)(2,1)S(1)} %copy-done.4), custom_call_target="tpu_custom_call" | custom-call | tf_op jit(solution)/shard_map/mix/pallas_call | solution.py:249
  30.7 0.0 copy-start
  30.7 0.0 copy-start.1
  30.7 0.0 copy-start.2
  30.7 0.0 copy-start.3
  30.7 20.8 %all_to_all.11 = f32[128,12,1,128]{3,2,1,0:T(1,128)S(1)} all-to-all(f32[128,12,1,128]{3,2,1,0:T(1,128)S(1)} %bitcast.7), channel_id=1, replica_groups=mesh['seq'=32,'ch'=4] {'ch','seq'}, dimensions={0} | all-to-all | bytes 1572864 | tf_op jit(solution)/shard_map/all_to_all | solution.py:244
  51.5 0.0 copy-done
  51.5 0.0 copy-done.1
  51.5 0.0 copy-done.2
  51.5 0.0 copy-done.3
  51.5 1.1 %unpack.1 = (bf16[512,128]{1,0:T(8,128)(2,1)}, bf16[512,128]{1,0:T(8,128)(2,1)}, bf16[512,128]{1,0:T(8,128)(2,1)}, bf16[512,128]{1,0:T(8,128)(2,1)}, f32[32,512]{1,0:T(8,128)}) custom-call(f32[1536,128]{1,0:T(8,128)S(1)} %bitcast.6, bf16[512,128]{1,0:T(8,128)(2,1)S(1)} %copy-done, bf16[512,128]{1,0:T(8,128)(2,1)S(1)} %copy-done.1, ...), custom_call_target="tpu_custom_call" | custom-call | tf_op jit(solution)/shard_map/unpack/pallas_call | solution.py:265
Async XLA Ops:
  2.0 25.6 %copy-start.4 = (bf16[2,256,256]{2,1,0:T(8,128)(2,1)S(1)}, bf16[2,256,256]{2,1,0:T(8,128)(2,1)}, u32[]{:S(2)}) copy-start(bf16[2,256,256]{2,1,0:T(8,128)(2,1)} %constant.14.clone.inverse) | copy-start | bytes 786436
  2.0 25.5 %copy-start.5 = (bf16[2,256,256]{2,1,0:T(8,128)(2,1)S(1)}, bf16[2,256,256]{2,1,0:T(8,128)(2,1)}, u32[]{:S(2)}) copy-start(bf16[2,256,256]{2,1,0:T(8,128)(2,1)} %constant.13.clone.forward) | copy-start | bytes 786436
  2.0 25.5 %copy-start.6 = (bf16[256,384]{1,0:T(8,128)(2,1)S(1)}, bf16[256,384]{1,0:T(8,128)(2,1)}, u32[]{:S(2)}) copy-start(bf16[256,384]{1,0:T(8,128)(2,1)} %constant.10.clone.first) | copy-start | bytes 589828
  2.0 25.5 %copy-start.7 = (f32[2,128,128]{2,1,0:T(8,128)S(1)}, f32[2,128,128]{2,1,0:T(8,128)}, u32[]{:S(2)}) copy-start(f32[2,128,128]{2,1,0:T(8,128)} %constant.12.clone.twist) | copy-start | bytes 393220
  2.0 25.5 %copy-start.8 = (bf16[2,128,256]{2,1,0:T(8,128)(2,1)S(1)}, bf16[2,128,256]{2,1,0:T(8,128)(2,1)}, u32[]{:S(2)}) copy-start(bf16[2,128,256]{2,1,0:T(8,128)(2,1)} %constant.11.clone.last) | copy-start | bytes 393220
  30.7 20.8 %copy-start = (bf16[512,128]{1,0:T(8,128)(2,1)S(1)}, bf16[512,128]{1,0:T(8,128)(2,1)}, u32[]{:S(2)}) copy-start(bf16[512,128]{1,0:T(8,128)(2,1)} %query.3) | copy-start | bytes 393220
  30.7 20.8 %copy-start.1 = (bf16[512,128]{1,0:T(8,128)(2,1)S(1)}, bf16[512,128]{1,0:T(8,128)(2,1)}, u32[]{:S(2)}) copy-start(bf16[512,128]{1,0:T(8,128)(2,1)} %key.3) | copy-start | bytes 393220
  30.7 20.8 %copy-start.2 = (bf16[512,128]{1,0:T(8,128)(2,1)S(1)}, bf16[512,128]{1,0:T(8,128)(2,1)}, u32[]{:S(2)}) copy-start(bf16[512,128]{1,0:T(8,128)(2,1)} %value.3) | copy-start | bytes 393220
  30.7 20.8 %copy-start.3 = (bf16[512,128]{1,0:T(8,128)(2,1)S(1)}, bf16[512,128]{1,0:T(8,128)(2,1)}, u32[]{:S(2)}) copy-start(bf16[512,128]{1,0:T(8,128)(2,1)} %grad.3) | copy-start | bytes 393220

commit v3 on v2

--- a/solution.py
+++ b/solution.py
@@ -18,6 +18,11 @@
     high = table.astype(BF16)
     low = (table - high.astype(np.float64)).astype(BF16)
     return high, low
+
+
+def stacked(pair):
+    high, low = pair
+    return np.concatenate([high, high, low], axis=0)
 
 
 @functools.lru_cache(maxsize=None)
@@ -36,9 +41,9 @@
     twist = np.stack([np.cos(turn), np.sin(turn)]).astype(np.float32)
     wave = -2.0 * np.pi * ((fine[:, None] * fine[None, :]) % FINE) / FINE
     re, im = np.cos(wave), np.sin(wave)
-    forward = np.stack(split_table(np.block([[re, im], [-im, re]])))
-    inverse = np.stack(split_table(np.block([[re, -im], [im, re]])))
-    return first_cat, np.stack([last_high, last_low]), twist, forward, inverse
+    stack = [stacked(split_table(np.block(parts))) for parts in ([[re, im], [-im, re]], [[re, -im], [im, re]])]
+    last_cat = np.concatenate([last_high, last_low], axis=0)
+    return first_cat, last_cat, twist, *stack
 
 
 def dot(left, right):
@@ -81,13 +86,10 @@
 
 
 def mix_kernel(
-    seq_count, pieces, rows_in, rows_out,
-    data, first, last, twist, forward, inverse,
-    out, part_high, part_low, spec, back_high, back_low,
+    seq_count, pieces, rows_in, rows_out, data, first, last, twist, forward, inverse, out,
 ):
     groups = pieces
     coarse = seq_count * pieces
-    signals = 2 * groups + 1
 
     def gather(start, step):
         return jnp.concatenate(
@@ -95,75 +97,76 @@
             axis=0,
         )
 
-    def load(index):
-        if index == 2 * groups:
-            return gather(2 * pieces, seq_count * rows_in)
-        group, kind = index % groups, index // groups
-        return gather(group * seq_count * rows_in + kind * pieces, 1)
-
-    twist_re, twist_im = twist[0], twist[1]
-    for begin in range(0, signals, 2):
-        members = range(begin, min(begin + 2, signals))
-        high, low = halves(jnp.concatenate([load(i) for i in members], axis=1))
-        mid = dot(first[...], jnp.concatenate([high, high, low], axis=0))
-        for place, index in enumerate(members):
-            cols = slice(FINE * place, FINE * place + FINE)
-            re, im = mid[:coarse, cols], mid[coarse:, cols]
-            turned_re = re * twist_re - im * twist_im
-            turned_im = re * twist_im + im * twist_re
-            rows = slice(coarse * index, coarse * index + coarse)
-            part_high[rows, :FINE], part_low[rows, :FINE] = halves(turned_re)
-            part_high[rows, FINE:], part_low[rows, FINE:] = halves(turned_im)
-
-    spec[...] = (
-        dot(part_high[...], forward[0]) + dot(part_low[...], forward[0]) + dot(part_high[...], forward[1])
-    )
-
-    def spectrum(index):
-        rows = slice(coarse * index, coarse * index + coarse)
-        return spec[rows, :FINE], spec[rows, FINE:]
-
-    def keep(index, re, im):
-        rows = slice(coarse * index, coarse * index + coarse)
-        part_high[rows, :FINE], part_low[rows, :FINE] = halves(re)
-        part_high[rows, FINE:], part_low[rows, FINE:] = halves(im)
-
-    taps_re, taps_im = spectrum(2 * groups)
-    corr_re = jnp.zeros_like(taps_re)
-    corr_im = jnp.zeros_like(taps_im)
+    def turn(re, im, sign):
+        turn_re, turn_im = twist[0], twist[1] * sign if sign < 0 else twist[1]
+        return re * turn_re - im * turn_im, re * turn_im + im * turn_re
+
+    def wave(parts, table):
+        pairs = [halves(jnp.concatenate(part, axis=1)) for part in parts]
+        high = jnp.concatenate([pair[0] for pair in pairs], axis=0)
+        low = jnp.concatenate([pair[1] for pair in pairs], axis=0)
+        count = high.shape[0]
+        both = dot(jnp.concatenate([high, low], axis=0), table[: 2 * FINE, :])
+        product = both[:count] + (both[count:] + dot(high, table[4 * FINE :, :]))
+        return [
+            (product[coarse * i : coarse * i + coarse, :FINE], product[coarse * i : coarse * i + coarse, FINE:])
+            for i in range(len(parts))
+        ]
+
+    def begin(signals):
+        high, low = halves(jnp.concatenate(signals, axis=1))
+        return dot(first[...], jnp.concatenate([high, high, low], axis=0))
+
+    def twisted(mid):
+        parts = []
+        for i in range(mid.shape[1] // FINE):
+            cols = slice(FINE * i, FINE * i + FINE)
+            parts.append(turn(mid[:coarse, cols], mid[coarse:, cols], 1))
+        return parts
+
+    def multiply(spectra):
+        (mixed_re, mixed_im), (grad_re, grad_im) = spectra
+        conv = (taps_re * mixed_re - taps_im * mixed_im, taps_re * mixed_im + taps_im * mixed_re)
+        back = (taps_re * grad_re + taps_im * grad_im, taps_re * grad_im - taps_im * grad_re)
+        corr = (mixed_re * grad_re + mixed_im * grad_im, mixed_re * grad_im - mixed_im * grad_re)
+        return conv, back, corr
+
+    def untwist(spectra):
+        return [turn(re, im, -1) for re, im in spectra]
+
+    def finish(parts):
+        pairs = [halves(jnp.concatenate(part, axis=0)) for part in parts]
+        high = jnp.concatenate([pair[0] for pair in pairs], axis=1)
+        low = jnp.concatenate([pair[1] for pair in pairs], axis=1)
+        both = dot(last[...], high)
+        result = both[:coarse] + (both[coarse:] + dot(last[:coarse, :], low))
+        return [result[:, FINE * i : FINE * i + FINE] for i in range(len(parts))]
+
+    def put(block, group, row):
+        for piece in range(pieces):
+            start = group * seq_count * rows_out + row + piece
+            out[pl.ds(start, seq_count, stride=rows_out), :] = block[
+                seq_count * piece : seq_count * piece + seq_count, :
+            ]
+
+    keys = ["t", *range(groups)]
+    load = {key: ([gather(2 * pieces, seq_count * rows_in)] if key == "t" else [gather(key * seq_count * rows_in, 1), gather(key * seq_count * rows_in + pieces, 1)]) for key in keys}
+    mids = {key: begin(load[key]) for key in keys}
+    parts = {key: twisted(mids[key]) for key in keys}
+    spectra = {key: wave(parts[key], forward) for key in keys}
+    ((taps_re, taps_im),) = spectra["t"]
+    products = {group: multiply(spectra[group]) for group in range(groups)}
+    corr = tuple(sum(products[group][2][part] for group in range(groups)) for part in range(2))
+    lists = {group: list(products[group][:2]) for group in range(groups)}
+    lists["t"] = [corr]
+    order = [*range(groups), "t"]
+    waves = {key: wave(lists[key], inverse) for key in order}
+    turned = {key: untwist(waves[key]) for key in order}
+    results = {key: finish(turned[key]) for key in order}
     for group in range(groups):
-        mixed_re, mixed_im = spectrum(group)
-        grad_re, grad_im = spectrum(groups + group)
-        keep(group, taps_re * mixed_re - taps_im * mixed_im, taps_re * mixed_im + taps_im * mixed_re)
-        keep(groups + group, taps_re * grad_re + taps_im * grad_im, taps_re * grad_im - taps_im * grad_re)
-        corr_re += mixed_re * grad_re + mixed_im * grad_im
-        corr_im += mixed_re * grad_im - mixed_im * grad_re
-    keep(2 * groups, corr_re, corr_im)
-
-    spec[...] = (
-        dot(part_high[...], inverse[0]) + dot(part_low[...], inverse[0]) + dot(part_high[...], inverse[1])
-    )
-    for index in range(signals):
-        re, im = spectrum(index)
-        cols = slice(FINE * index, FINE * index + FINE)
-        back_high[:coarse, cols], back_low[:coarse, cols] = halves(re * twist_re + im * twist_im)
-        back_high[coarse:, cols], back_low[coarse:, cols] = halves(im * twist_re - re * twist_im)
-
-    for index in range(signals):
-        cols = slice(FINE * index, FINE * index + FINE)
-        result = (
-            dot(last[0], back_high[:, cols]) + dot(last[0], back_low[:, cols]) + dot(last[1], back_high[:, cols])
-        )
-        for piece in range(pieces):
-            block = result[seq_count * piece : seq_count * piece + seq_count, :]
-            if index == 2 * groups:
-                for group in range(groups):
-                    start = group * seq_count * rows_out + 2 * pieces + piece
-                    out[pl.ds(start, seq_count, stride=rows_out), :] = block
-            else:
-                group, kind = index % groups, index // groups
-                start = group * seq_count * rows_out + kind * pieces + piece
-                out[pl.ds(start, seq_count, stride=rows_out), :] = block
+        for kind, block in enumerate(results[group]):
+            put(block, group, kind * pieces)
+        put(results["t"][0], group, 2 * pieces)
 
 
 def unpack_kernel(
@@ -220,8 +223,6 @@
     rows_in = 2 * pieces + 1
     rows_out = 3 * pieces
     seq_total = local_rows * seq_count
-    coarse = seq_count * pieces
-    signals = 2 * groups + 1
 
     hbm = pl.BlockSpec(memory_space=pltpu.HBM)
     vmem = pl.BlockSpec(memory_space=pltpu.VMEM)
@@ -249,13 +250,6 @@
     mixed = pl.pallas_call(
         functools.partial(mix_kernel, seq_count, pieces, rows_in, rows_out),
         out_shape=jax.ShapeDtypeStruct((devices * rows_out, FINE), F32),
-        scratch_shapes=[
-            pltpu.VMEM((signals * coarse, 2 * FINE), BF16),
-            pltpu.VMEM((signals * coarse, 2 * FINE), BF16),
-            pltpu.VMEM((signals * coarse, 2 * FINE), F32),
-            pltpu.VMEM((2 * coarse, signals * FINE), BF16),
-            pltpu.VMEM((2 * coarse, signals * FINE), BF16),
-        ],
         compiler_params=pltpu.CompilerParams(vmem_limit_bytes=24 << 20),
         name="mix",
     )(gathered, *constants)

time: 52.7 us -> 51.4 us (0.975)
  Pallas kernels: 5.49 us -> 4.16 us
    pallas_call x1, Pallas kernels: 3.08 us -> 1.73 us  [local(): pl.pallas_call(functools.partial(mix_kernel, seq_count, pieces, rows_in,...]
where the time goes in v3:
time: 51.4 us; the launch traced here: 51.2 us
  blocking collectives  46.2 us (90%)
  Pallas kernels  4.16 us (8%)
  between operations  0.75 us (1%)
    all_to_all x2, blocking collectives, exchange(): array = lax.all_to_all(array, ('ch', 'seq'), 0, 0, tiled=True)  46.2 us
    pallas_call x1, Pallas kernels, local(): pl.pallas_call(functools.partial(mix_kernel, seq_count, pieces, rows_in,...  1.73 us
    pallas_call x1, Pallas kernels, local(): pl.pallas_call(functools.partial(pack_kernel, pieces, rows_in), out_shape...  1.37 us
    pallas_call x1, Pallas kernels, local(): pl.pallas_call(functools.partial(unpack_kernel, pieces, rows_out, 1.0 / m...  1.06 us

profile of v3, /device:TPU:1, one launch (start us, length us, event | category | flops | bytes accessed | tf_op | source)
XLA Modules:
  0.0 51.2 jit_solution(11115057145170536452)
XLA Ops:
  0.6 0.0 copy-start.8
  0.6 1.4 %pack.1 = (f32[1152,128]{1,0:T(8,128)S(1)}, f32[1,128]{1,0:T(1,128)S(1)}) custom-call(bf16[512,128]{1,0:T(8,128)(2,1)} %query.3, bf16[512,128]{1,0:T(8,128)(2,1)} %key.3, bf16[512,128]{1,0:T(8,128)(2,1)} %value.3, bf16[512,128]{1,0:T(8,128)(2,1)} %grad.3, f32[512,128]{1,0:T(8,128)} %taps.1, f32[1,128]{1,0:T(1,128)} %bitcast.10), custom_call_target="tpu_custom_call" | custom-call | tf_op jit(solution)/shard_map/pack/pallas_call | solution.py:230
  2.0 0.0 copy-start.4
  2.0 0.0 copy-start.5
  2.0 0.0 copy-start.6
  2.1 0.0 copy-start.7
  2.1 25.5 %all_to_all.10 = f32[128,9,1,128]{3,2,1,0:T(1,128)S(1)} all-to-all(f32[128,9,1,128]{3,2,1,0:T(1,128)S(1)} %bitcast.9), channel_id=1, replica_groups=mesh['seq'=32,'ch'=4] {'ch','seq'}, dimensions={0} | all-to-all | bytes 1179648 | tf_op jit(solution)/shard_map/all_to_all | solution.py:245
  27.6 0.0 copy-done.8
  27.6 0.0 copy-done.4
  27.6 0.0 copy-done.5
  27.6 0.0 copy-done.6
  27.6 0.0 copy-done.7
  27.6 1.7 %mix.1 = f32[1536,128]{1,0:T(8,128)S(1)} custom-call(f32[1152,128]{1,0:T(8,128)S(1)} %bitcast.8, bf16[256,384]{1,0:T(8,128)(2,1)S(1)} %copy-done.6, bf16[256,256]{1,0:T(8,128)(2,1)S(1)} %copy-done.8, f32[2,128,128]{2,1,0:T(8,128)S(1)} %copy-done.7, bf16[768,256]{1,0:T(8,128)(2,1)S(1)} %copy-done.5, bf16[768,256]{1,0:T(8,128)(2,1)S(1)} %copy-done.4), custom_call_target="tpu_custom_call" | custom-call | tf_op jit(solution)/shard_map/mix/pallas_call | solution.py:250
  29.3 0.0 copy-start
  29.3 0.0 copy-start.1
  29.4 0.0 copy-start.2
  29.4 0.0 copy-start.3
  29.4 20.8 %all_to_all.11 = f32[128,12,1,128]{3,2,1,0:T(1,128)S(1)} all-to-all(f32[128,12,1,128]{3,2,1,0:T(1,128)S(1)} %bitcast.7), channel_id=1, replica_groups=mesh['seq'=32,'ch'=4] {'ch','seq'}, dimensions={0} | all-to-all | bytes 1572864 | tf_op jit(solution)/shard_map/all_to_all | solution.py:245
  50.1 0.0 copy-done
  50.1 0.0 copy-done.1
  50.1 0.0 copy-done.2
  50.1 0.0 copy-done.3
  50.2 1.1 %unpack.1 = (bf16[512,128]{1,0:T(8,128)(2,1)}, bf16[512,128]{1,0:T(8,128)(2,1)}, bf16[512,128]{1,0:T(8,128)(2,1)}, bf16[512,128]{1,0:T(8,128)(2,1)}, f32[32,512]{1,0:T(8,128)}) custom-call(f32[1536,128]{1,0:T(8,128)S(1)} %bitcast.6, bf16[512,128]{1,0:T(8,128)(2,1)S(1)} %copy-done, bf16[512,128]{1,0:T(8,128)(2,1)S(1)} %copy-done.1, ...), custom_call_target="tpu_custom_call" | custom-call | tf_op jit(solution)/shard_map/unpack/pallas_call | solution.py:259
Async XLA Ops:
  0.6 26.9 %copy-start.8 = (bf16[256,256]{1,0:T(8,128)(2,1)S(1)}, bf16[256,256]{1,0:T(8,128)(2,1)}, u32[]{:S(2)}) copy-start(bf16[256,256]{1,0:T(8,128)(2,1)} %constant.11.clone.last) | copy-start | bytes 393220
  2.0 25.5 %copy-start.4 = (bf16[768,256]{1,0:T(8,128)(2,1)S(1)}, bf16[768,256]{1,0:T(8,128)(2,1)}, u32[]{:S(2)}) copy-start(bf16[768,256]{1,0:T(8,128)(2,1)} %constant.14.clone.inverse) | copy-start | bytes 1179652
  2.0 25.5 %copy-start.5 = (bf16[768,256]{1,0:T(8,128)(2,1)S(1)}, bf16[768,256]{1,0:T(8,128)(2,1)}, u32[]{:S(2)}) copy-start(bf16[768,256]{1,0:T(8,128)(2,1)} %constant.13.clone.forward) | copy-start | bytes 1179652
  2.0 25.5 %copy-start.6 = (bf16[256,384]{1,0:T(8,128)(2,1)S(1)}, bf16[256,384]{1,0:T(8,128)(2,1)}, u32[]{:S(2)}) copy-start(bf16[256,384]{1,0:T(8,128)(2,1)} %constant.10.clone.first) | copy-start | bytes 589828
  2.1 25.5 %copy-start.7 = (f32[2,128,128]{2,1,0:T(8,128)S(1)}, f32[2,128,128]{2,1,0:T(8,128)}, u32[]{:S(2)}) copy-start(f32[2,128,128]{2,1,0:T(8,128)} %constant.12.clone.twist) | copy-start | bytes 393220
  29.3 20.8 %copy-start = (bf16[512,128]{1,0:T(8,128)(2,1)S(1)}, bf16[512,128]{1,0:T(8,128)(2,1)}, u32[]{:S(2)}) copy-start(bf16[512,128]{1,0:T(8,128)(2,1)} %query.3) | copy-start | bytes 393220
  29.3 20.8 %copy-start.1 = (bf16[512,128]{1,0:T(8,128)(2,1)S(1)}, bf16[512,128]{1,0:T(8,128)(2,1)}, u32[]{:S(2)}) copy-start(bf16[512,128]{1,0:T(8,128)(2,1)} %key.3) | copy-start | bytes 393220
  29.4 20.8 %copy-start.2 = (bf16[512,128]{1,0:T(8,128)(2,1)S(1)}, bf16[512,128]{1,0:T(8,128)(2,1)}, u32[]{:S(2)}) copy-start(bf16[512,128]{1,0:T(8,128)(2,1)} %value.3) | copy-start | bytes 393220
  29.4 20.8 %copy-start.3 = (bf16[512,128]{1,0:T(8,128)(2,1)S(1)}, bf16[512,128]{1,0:T(8,128)(2,1)}, u32[]{:S(2)}) copy-start(bf16[512,128]{1,0:T(8,128)(2,1)} %grad.3) | copy-start | bytes 393220

commit v4 on v3

--- a/solution.py
+++ b/solution.py
@@ -55,19 +55,17 @@
     return high, (value - high.astype(F32)).astype(BF16)
 
 
-def pack_kernel(pieces, rows_per, query, key, value, grad, taps, gain, out, gain_out, *scratch):
+def pack_kernel(pieces, rows_per, query, key, value, grad, taps, out, *scratch):
     query_in, key_in, value_in, grad_in, taps_in, sems = scratch
     own = lax.axis_index("ch")
     count = out.shape[0] // rows_per
     rows = pl.ds(pl.multiple_of(own * FINE, FINE), FINE)
     taps_copy = pltpu.make_async_copy(taps.at[rows, :], taps_in, sems.at[4])
-    gain_copy = pltpu.make_async_copy(gain, gain_out, sems.at[5])
     pairs = ((key, key_in), (value, value_in), (grad, grad_in), (query, query_in))
     copies = [pltpu.make_async_copy(src, dst, sems.at[i]) for i, (src, dst) in enumerate(pairs)]
     taps_copy.start()
     for copy in copies:
         copy.start()
-    gain_copy.start()
     taps_copy.wait()
     out[pl.ds(2 * pieces, count, stride=rows_per), :] = taps_in[...].T
     copies[0].wait()
@@ -82,14 +80,15 @@
         rows = pl.ds(FINE * piece, FINE)
         grads = grad_in[rows, :].astype(F32) * query_in[rows, :].astype(F32)
         out[pl.ds(pieces + piece, count, stride=rows_per), :] = grads.T
-    gain_copy.wait()
 
 
 def mix_kernel(
-    seq_count, pieces, rows_in, rows_out, data, first, last, twist, forward, inverse, out,
+    seq_count, pieces, rows_in, rows_out, data, first, last, twist, forward, inverse, gain, out, gain_out, gain_sem,
 ):
     groups = pieces
     coarse = seq_count * pieces
+    gain_copy = pltpu.make_async_copy(gain, gain_out, gain_sem)
+    gain_copy.start()
 
     def gather(start, step):
         return jnp.concatenate(
@@ -167,6 +166,7 @@
         for kind, block in enumerate(results[group]):
             put(block, group, kind * pieces)
         put(results["t"][0], group, 2 * pieces)
+    gain_copy.wait()
 
 
 def unpack_kernel(
@@ -178,36 +178,31 @@
     count = data.shape[0] // rows_per
     owned = grad_filter.shape[0]
     gain_row = gain[...]
-    copies = []
-
-    def send(index, piece, target):
-        rows = pl.ds(FINE * piece, FINE)
-        copy = pltpu.make_async_copy(holds[index].at[rows, :], target.at[rows, :], sems.at[index, piece])
-        copy.start()
-        copies.append(copy)
-
+    targets = (mixer_out, grad_query, grad_key, grad_value)
+    copies = [pltpu.make_async_copy(holds[i], targets[i], sems.at[i]) for i in range(4)]
+    copies.append(pltpu.make_async_copy(filter_hold, grad_filter, sems.at[4]))
+    for piece in range(pieces):
+        rows = pl.ds(FINE * piece, FINE)
+        mixed = key[rows, :].astype(F32) * value[rows, :].astype(F32)
+        conv = data[pl.ds(piece, count, stride=rows_per), :].T
+        pre = conv + gain_row * mixed
+        holds[0][rows, :] = (query[rows, :].astype(F32) * pre).astype(BF16)
+        holds[1][rows, :] = (grad[rows, :].astype(F32) * pre).astype(BF16)
+    copies[0].start()
+    copies[1].start()
+    for piece in range(pieces):
+        rows = pl.ds(FINE * piece, FINE)
+        upstream = grad[rows, :].astype(F32) * query[rows, :].astype(F32)
+        corr = data[pl.ds(pieces + piece, count, stride=rows_per), :].T
+        back = corr + gain_row * upstream
+        holds[2][rows, :] = (back * value[rows, :].astype(F32)).astype(BF16)
+        holds[3][rows, :] = (back * key[rows, :].astype(F32)).astype(BF16)
+    copies[2].start()
+    copies[3].start()
     for piece in range(pieces):
         start = own * (owned * rows_per) + 2 * pieces + piece
         filter_hold[:, FINE * piece : FINE * piece + FINE] = data[pl.ds(start, owned, stride=rows_per), :] * scale
-    filter_copy = pltpu.make_async_copy(filter_hold, grad_filter, sems.at[4, 0])
-    filter_copy.start()
-    for piece in range(pieces):
-        rows = pl.ds(FINE * piece, FINE)
-        query_data, key_data = query[rows, :].astype(F32), key[rows, :].astype(F32)
-        value_data, upstream = value[rows, :].astype(F32), grad[rows, :].astype(F32)
-        conv = data[pl.ds(piece, count, stride=rows_per), :].T
-        pre = conv + gain_row * (key_data * value_data)
-        holds[0][rows, :] = (query_data * pre).astype(BF16)
-        send(0, piece, mixer_out)
-        holds[1][rows, :] = (upstream * pre).astype(BF16)
-        send(1, piece, grad_query)
-        corr = data[pl.ds(pieces + piece, count, stride=rows_per), :].T
-        back = corr + gain_row * (upstream * query_data)
-        holds[2][rows, :] = (back * value_data).astype(BF16)
-        send(2, piece, grad_key)
-        holds[3][rows, :] = (back * key_data).astype(BF16)
-        send(3, piece, grad_value)
-    filter_copy.wait()
+    copies[4].start()
     for copy in copies:
         copy.wait()
 
@@ -227,18 +222,15 @@
     hbm = pl.BlockSpec(memory_space=pltpu.HBM)
     vmem = pl.BlockSpec(memory_space=pltpu.VMEM)
     half = pltpu.VMEM((local_rows, local_ch), BF16)
-    packed, gain_row = pl.pallas_call(
+    packed = pl.pallas_call(
         functools.partial(pack_kernel, pieces, rows_in),
-        out_shape=(
-            jax.ShapeDtypeStruct((devices * rows_in, FINE), F32),
-            jax.ShapeDtypeStruct((1, local_ch), F32),
-        ),
-        in_specs=[hbm] * 6,
-        out_specs=(vmem, vmem),
-        scratch_shapes=[half] * 4 + [pltpu.VMEM((FINE, local_ch), F32), pltpu.SemaphoreType.DMA((6,))],
+        out_shape=jax.ShapeDtypeStruct((devices * rows_in, FINE), F32),
+        in_specs=[hbm] * 5,
+        out_specs=vmem,
+        scratch_shapes=[half] * 4 + [pltpu.VMEM((FINE, local_ch), F32), pltpu.SemaphoreType.DMA((5,))],
         compiler_params=pltpu.CompilerParams(vmem_limit_bytes=8 << 20),
         name="pack",
-    )(*[pltpu.with_memory_space_constraint(x, pltpu.HBM) for x in (query_proj, key_proj, value_proj, grad_mixer, filter_taps, skip_gain[None, :])])
+    )(*[pltpu.with_memory_space_constraint(x, pltpu.HBM) for x in (query_proj, key_proj, value_proj, grad_mixer, filter_taps)])
 
     def exchange(array, rows):
         array = array.reshape(devices, rows, 1, FINE)
@@ -247,12 +239,18 @@
 
     gathered = exchange(packed, rows_in)
     constants = [jnp.asarray(table) for table in tables(seq_count, pieces)]
-    mixed = pl.pallas_call(
+    mixed, gain_row = pl.pallas_call(
         functools.partial(mix_kernel, seq_count, pieces, rows_in, rows_out),
-        out_shape=jax.ShapeDtypeStruct((devices * rows_out, FINE), F32),
+        out_shape=(
+            jax.ShapeDtypeStruct((devices * rows_out, FINE), F32),
+            jax.ShapeDtypeStruct((1, local_ch), F32),
+        ),
+        in_specs=[vmem] * 6 + [hbm],
+        out_specs=(vmem, vmem),
+        scratch_shapes=[pltpu.SemaphoreType.DMA],
         compiler_params=pltpu.CompilerParams(vmem_limit_bytes=24 << 20),
         name="mix",
-    )(gathered, *constants)
+    )(gathered, *constants, pltpu.with_memory_space_constraint(skip_gain[None, :], pltpu.HBM))
     returned = exchange(mixed, rows_out)
 
     out_bf16 = jax.ShapeDtypeStruct((local_rows, local_ch), BF16)
@@ -265,7 +263,7 @@
         in_specs=[vmem] * 6,
         out_specs=(hbm,) * 5,
         scratch_shapes=[half] * 4
-        + [pltpu.VMEM((local_ch // ch_count, local_rows), F32), pltpu.SemaphoreType.DMA((5, pieces))],
+        + [pltpu.VMEM((local_ch // ch_count, local_rows), F32), pltpu.SemaphoreType.DMA((5,))],
         compiler_params=pltpu.CompilerParams(vmem_limit_bytes=8 << 20),
         name="unpack",
     )(returned, query_proj, key_proj, value_proj, grad_mixer, gain_row)

time: 51.4 us -> 51.3 us (level)
  no operation moved by 1% of the time
where the time goes in v4:
time: 51.3 us; the launch traced here: 51.2 us
  blocking collectives  46.2 us (90%)
  Pallas kernels  4.1 us (8%)
  between operations  0.75 us (1%)
    all_to_all x2, blocking collectives, exchange(): array = lax.all_to_all(array, ('ch', 'seq'), 0, 0, tiled=True)  46.2 us
    pallas_call x1, Pallas kernels, local(): pl.pallas_call(functools.partial(mix_kernel, seq_count, pieces, rows_in,...  1.74 us
    pallas_call x1, Pallas kernels, local(): pl.pallas_call(functools.partial(pack_kernel, pieces, rows_in), out_shape...  1.36 us

profile of v4, /device:TPU:1, one launch (start us, length us, event | category | flops | bytes accessed | tf_op | source)
XLA Modules:
  0.0 51.2 jit_solution(1380632417782562777)
XLA Ops:
  0.6 0.0 copy-start.8
  0.6 1.4 %pack.1 = f32[1152,128]{1,0:T(8,128)S(1)} custom-call(bf16[512,128]{1,0:T(8,128)(2,1)} %query.3, bf16[512,128]{1,0:T(8,128)(2,1)} %key.3, bf16[512,128]{1,0:T(8,128)(2,1)} %value.3, bf16[512,128]{1,0:T(8,128)(2,1)} %grad.3, f32[512,128]{1,0:T(8,128)} %taps.1), custom_call_target="tpu_custom_call" | custom-call | tf_op jit(solution)/shard_map/pack/pallas_call | solution.py:225
  2.0 0.0 copy-start.4
  2.0 0.0 copy-start.5
  2.0 0.0 copy-start.6
  2.1 0.0 copy-start.7
  2.1 25.5 %all_to_all.10 = f32[128,9,1,128]{3,2,1,0:T(1,128)S(1)} all-to-all(f32[128,9,1,128]{3,2,1,0:T(1,128)S(1)} %bitcast.8), channel_id=1, replica_groups=mesh['seq'=32,'ch'=4] {'ch','seq'}, dimensions={0} | all-to-all | bytes 1179648 | tf_op jit(solution)/shard_map/all_to_all | solution.py:237
  27.6 0.0 copy-done.8
  27.6 0.0 copy-done.4
  27.6 0.0 copy-done.5
  27.6 0.0 copy-done.6
  27.6 0.0 copy-done.7
  27.6 1.7 %mix.1 = (f32[1536,128]{1,0:T(8,128)S(1)}, f32[1,128]{1,0:T(1,128)S(1)}) custom-call(f32[1152,128]{1,0:T(8,128)S(1)} %bitcast.7, bf16[256,384]{1,0:T(8,128)(2,1)S(1)} %copy-done.6, bf16[256,256]{1,0:T(8,128)(2,1)S(1)} %copy-done.8, f32[2,128,128]{2,1,0:T(8,128)S(1)} %copy-done.7, bf16[768,256]{1,0:T(8,128)(2,1)S(1)} %copy-done.5, ...), custom_call_target="tpu_custom_call" | custom-call | tf_op jit(solution)/shard_map/mix/pallas_call | solution.py:242
  29.3 0.0 copy-start
  29.3 0.0 copy-start.1
  29.4 0.0 copy-start.2
  29.4 0.0 copy-start.3
  29.4 20.8 %all_to_all.11 = f32[128,12,1,128]{3,2,1,0:T(1,128)S(1)} all-to-all(f32[128,12,1,128]{3,2,1,0:T(1,128)S(1)} %bitcast.9), channel_id=1, replica_groups=mesh['seq'=32,'ch'=4] {'ch','seq'}, dimensions={0} | all-to-all | bytes 1572864 | tf_op jit(solution)/shard_map/all_to_all | solution.py:237
  50.1 0.0 copy-done
  50.1 0.0 copy-done.1
  50.2 0.0 copy-done.2
  50.2 0.0 copy-done.3
  50.2 1.0 %unpack.1 = (bf16[512,128]{1,0:T(8,128)(2,1)}, bf16[512,128]{1,0:T(8,128)(2,1)}, bf16[512,128]{1,0:T(8,128)(2,1)}, bf16[512,128]{1,0:T(8,128)(2,1)}, f32[32,512]{1,0:T(8,128)}) custom-call(f32[1536,128]{1,0:T(8,128)S(1)} %bitcast.6, bf16[512,128]{1,0:T(8,128)(2,1)S(1)} %copy-done, bf16[512,128]{1,0:T(8,128)(2,1)S(1)} %copy-done.1, ...), custom_call_target="tpu_custom_call" | custom-call | tf_op jit(solution)/shard_map/unpack/pallas_call | solution.py:257
Async XLA Ops:
  0.6 26.9 %copy-start.8 = (bf16[256,256]{1,0:T(8,128)(2,1)S(1)}, bf16[256,256]{1,0:T(8,128)(2,1)}, u32[]{:S(2)}) copy-start(bf16[256,256]{1,0:T(8,128)(2,1)} %constant.11.clone.last) | copy-start | bytes 393220
  2.0 25.5 %copy-start.4 = (bf16[768,256]{1,0:T(8,128)(2,1)S(1)}, bf16[768,256]{1,0:T(8,128)(2,1)}, u32[]{:S(2)}) copy-start(bf16[768,256]{1,0:T(8,128)(2,1)} %constant.14.clone.inverse) | copy-start | bytes 1179652
  2.0 25.5 %copy-start.5 = (bf16[768,256]{1,0:T(8,128)(2,1)S(1)}, bf16[768,256]{1,0:T(8,128)(2,1)}, u32[]{:S(2)}) copy-start(bf16[768,256]{1,0:T(8,128)(2,1)} %constant.13.clone.forward) | copy-start | bytes 1179652
  2.0 25.5 %copy-start.6 = (bf16[256,384]{1,0:T(8,128)(2,1)S(1)}, bf16[256,384]{1,0:T(8,128)(2,1)}, u32[]{:S(2)}) copy-start(bf16[256,384]{1,0:T(8,128)(2,1)} %constant.10.clone.first) | copy-start | bytes 589828
  2.1 25.5 %copy-start.7 = (f32[2,128,128]{2,1,0:T(8,128)S(1)}, f32[2,128,128]{2,1,0:T(8,128)}, u32[]{:S(2)}) copy-start(f32[2,128,128]{2,1,0:T(8,128)} %constant.12.clone.twist) | copy-start | bytes 393220
  29.3 20.8 %copy-start = (bf16[512,128]{1,0:T(8,128)(2,1)S(1)}, bf16[512,128]{1,0:T(8,128)(2,1)}, u32[]{:S(2)}) copy-start(bf16[512,128]{1,0:T(8,128)(2,1)} %query.3) | copy-start | bytes 393220
  29.3 20.8 %copy-start.1 = (bf16[512,128]{1,0:T(8,128)(2,1)S(1)}, bf16[512,128]{1,0:T(8,128)(2,1)}, u32[]{:S(2)}) copy-start(bf16[512,128]{1,0:T(8,128)(2,1)} %key.3) | copy-start | bytes 393220
  29.4 20.8 %copy-start.2 = (bf16[512,128]{1,0:T(8,128)(2,1)S(1)}, bf16[512,128]{1,0:T(8,128)(2,1)}, u32[]{:S(2)}) copy-start(bf16[512,128]{1,0:T(8,128)(2,1)} %value.3) | copy-start | bytes 393220
  29.4 20.8 %copy-start.3 = (bf16[512,128]{1,0:T(8,128)(2,1)S(1)}, bf16[512,128]{1,0:T(8,128)(2,1)}, u32[]{:S(2)}) copy-start(bf16[512,128]{1,0:T(8,128)(2,1)} %grad.3) | copy-start | bytes 393220

commit v5 on v4

--- a/solution.py
+++ b/solution.py
@@ -30,12 +30,16 @@
     coarse = seq_count * pieces
     total = coarse * FINE
     order = (pieces * np.arange(seq_count)[None, :] + np.arange(pieces)[:, None]).reshape(-1)
-    low = np.arange(coarse) + 0.5
+    low = np.concatenate([np.arange(coarse // 2), coarse - 1 - np.arange(coarse // 2)]) + 0.5
     fine = np.arange(FINE)
     angle = -2.0 * np.pi * low[:, None] * order[None, :] / (2 * coarse)
     first = np.concatenate([np.cos(angle), np.sin(angle)], axis=0)
-    first_high, first_low = split_table(first)
-    first_cat = np.concatenate([first_high, first_low, first_high], axis=1)
+    first_cat = []
+    for parity in range(2):
+        half = first[:, order % 2 == parity]
+        half_high, half_low = split_table(np.concatenate([half[: coarse // 2], half[coarse : coarse + coarse // 2]]))
+        first_cat.append(np.concatenate([half_high, half_low, half_high], axis=1))
+    first_cat = np.stack(first_cat)
     last_high, last_low = split_table(first.T / total)
     turn = -2.0 * np.pi * low[:, None] * fine[None, :] / (2 * total)
     twist = np.stack([np.cos(turn), np.sin(turn)]).astype(np.float32)
@@ -113,8 +117,24 @@
         ]
 
     def begin(signals):
-        high, low = halves(jnp.concatenate(signals, axis=1))
-        return dot(first[...], jnp.concatenate([high, high, low], axis=0))
+        sums = []
+        for parity in range(2):
+            part = jnp.concatenate(
+                [
+                    jnp.concatenate(
+                        [signal[seq_count * p : seq_count * p + seq_count] for p in range(parity, pieces, 2)], axis=0
+                    )
+                    for signal in signals
+                ],
+                axis=1,
+            )
+            high, low = halves(part)
+            sums.append(dot(first[parity], jnp.concatenate([high, high, low], axis=0)))
+        even, odd = sums
+        mid = coarse // 2
+        return jnp.concatenate(
+            [even[:mid] + odd[:mid], even[:mid] - odd[:mid], even[mid:] + odd[mid:], odd[mid:] - even[mid:]], axis=0
+        )
 
     def twisted(mid):
         parts = []

time: 51.3 us -> 51.2 us (level)
  no operation moved by 1% of the time
where the time goes in v5:
time: 51.2 us; the launch traced here: 51.1 us
  blocking collectives  46.2 us (90%)
  Pallas kernels  3.99 us (8%)
  between operations  0.75 us (1%)
    all_to_all x2, blocking collectives, exchange(): array = lax.all_to_all(array, ('ch', 'seq'), 0, 0, tiled=True)  46.2 us
    pallas_call x1, Pallas kernels, local(): pl.pallas_call(functools.partial(mix_kernel, seq_count, pieces, rows_in,...  1.66 us
    pallas_call x1, Pallas kernels, local(): pl.pallas_call(functools.partial(pack_kernel, pieces, rows_in), out_shape...  1.34 us

profile of v5, /device:TPU:1, one launch (start us, length us, event | category | flops | bytes accessed | tf_op | source)
XLA Modules:
  0.0 51.1 jit_solution(15478921634463353691)
XLA Ops:
  0.6 1.3 %pack.1 = f32[1152,128]{1,0:T(8,128)S(1)} custom-call(bf16[512,128]{1,0:T(8,128)(2,1)} %query.3, bf16[512,128]{1,0:T(8,128)(2,1)} %key.3, bf16[512,128]{1,0:T(8,128)(2,1)} %value.3, bf16[512,128]{1,0:T(8,128)(2,1)} %grad.3, f32[512,128]{1,0:T(8,128)} %taps.1), custom_call_target="tpu_custom_call" | custom-call | tf_op jit(solution)/shard_map/pack/pallas_call | solution.py:245
  2.0 0.0 copy-start.4
  2.0 0.0 copy-start.5
  2.0 0.0 copy-start.6
  2.0 0.0 copy-start.7
  2.0 0.0 copy-start.8
  2.0 25.5 %all_to_all.10 = f32[128,9,1,128]{3,2,1,0:T(1,128)S(1)} all-to-all(f32[128,9,1,128]{3,2,1,0:T(1,128)S(1)} %bitcast.8), channel_id=1, replica_groups=mesh['seq'=32,'ch'=4] {'ch','seq'}, dimensions={0} | all-to-all | bytes 1179648 | tf_op jit(solution)/shard_map/all_to_all | solution.py:257
  27.5 0.0 copy-done.4
  27.5 0.0 copy-done.5
  27.5 0.0 copy-done.6
  27.5 0.0 copy-done.7
  27.5 0.0 copy-done.8
  27.6 1.7 %mix.1 = (f32[1536,128]{1,0:T(8,128)S(1)}, f32[1,128]{1,0:T(1,128)S(1)}) custom-call(f32[1152,128]{1,0:T(8,128)S(1)} %bitcast.7, bf16[2,128,192]{2,1,0:T(8,128)(2,1)S(1)} %copy-done.8, bf16[256,256]{1,0:T(8,128)(2,1)S(1)} %copy-done.7, f32[2,128,128]{2,1,0:T(8,128)S(1)} %copy-done.6, bf16[768,256]{1,0:T(8,128)(2,1)S(1)} %copy-done.5, ...), custom_call_target="tpu_custom_call" | custom-call | tf_op jit(solution)/shard_map/mix/pallas_call | solution.py:262
  29.2 0.0 copy-start
  29.2 0.0 copy-start.1
  29.3 0.0 copy-start.2
  29.3 0.0 copy-start.3
  29.3 20.8 %all_to_all.11 = f32[128,12,1,128]{3,2,1,0:T(1,128)S(1)} all-to-all(f32[128,12,1,128]{3,2,1,0:T(1,128)S(1)} %bitcast.9), channel_id=1, replica_groups=mesh['seq'=32,'ch'=4] {'ch','seq'}, dimensions={0} | all-to-all | bytes 1572864 | tf_op jit(solution)/shard_map/all_to_all | solution.py:257
  50.0 0.0 copy-done
  50.0 0.0 copy-done.1
  50.0 0.0 copy-done.2
  50.0 0.0 copy-done.3
  50.1 1.0 %unpack.1 = (bf16[512,128]{1,0:T(8,128)(2,1)}, bf16[512,128]{1,0:T(8,128)(2,1)}, bf16[512,128]{1,0:T(8,128)(2,1)}, bf16[512,128]{1,0:T(8,128)(2,1)}, f32[32,512]{1,0:T(8,128)}) custom-call(f32[1536,128]{1,0:T(8,128)S(1)} %bitcast.6, bf16[512,128]{1,0:T(8,128)(2,1)S(1)} %copy-done, bf16[512,128]{1,0:T(8,128)(2,1)S(1)} %copy-done.1, ...), custom_call_target="tpu_custom_call" | custom-call | tf_op jit(solution)/shard_map/unpack/pallas_call | solution.py:277
Async XLA Ops:
  2.0 25.6 %copy-start.4 = (bf16[768,256]{1,0:T(8,128)(2,1)S(1)}, bf16[768,256]{1,0:T(8,128)(2,1)}, u32[]{:S(2)}) copy-start(bf16[768,256]{1,0:T(8,128)(2,1)} %constant.14.clone.inverse) | copy-start | bytes 1179652
  2.0 25.5 %copy-start.5 = (bf16[768,256]{1,0:T(8,128)(2,1)S(1)}, bf16[768,256]{1,0:T(8,128)(2,1)}, u32[]{:S(2)}) copy-start(bf16[768,256]{1,0:T(8,128)(2,1)} %constant.13.clone.forward) | copy-start | bytes 1179652
  2.0 25.5 %copy-start.6 = (f32[2,128,128]{2,1,0:T(8,128)S(1)}, f32[2,128,128]{2,1,0:T(8,128)}, u32[]{:S(2)}) copy-start(f32[2,128,128]{2,1,0:T(8,128)} %constant.12.clone.twist) | copy-start | bytes 393220
  2.0 25.5 %copy-start.7 = (bf16[256,256]{1,0:T(8,128)(2,1)S(1)}, bf16[256,256]{1,0:T(8,128)(2,1)}, u32[]{:S(2)}) copy-start(bf16[256,256]{1,0:T(8,128)(2,1)} %constant.11.clone.last) | copy-start | bytes 393220
  2.0 25.5 %copy-start.8 = (bf16[2,128,192]{2,1,0:T(8,128)(2,1)S(1)}, bf16[2,128,192]{2,1,0:T(8,128)(2,1)}, u32[]{:S(2)}) copy-start(bf16[2,128,192]{2,1,0:T(8,128)(2,1)} %constant.10.clone.first) | copy-start | bytes 294916
  29.2 20.8 %copy-start = (bf16[512,128]{1,0:T(8,128)(2,1)S(1)}, bf16[512,128]{1,0:T(8,128)(2,1)}, u32[]{:S(2)}) copy-start(bf16[512,128]{1,0:T(8,128)(2,1)} %query.3) | copy-start | bytes 393220
  29.2 20.8 %copy-start.1 = (bf16[512,128]{1,0:T(8,128)(2,1)S(1)}, bf16[512,128]{1,0:T(8,128)(2,1)}, u32[]{:S(2)}) copy-start(bf16[512,128]{1,0:T(8,128)(2,1)} %key.3) | copy-start | bytes 393220
  29.3 20.8 %copy-start.2 = (bf16[512,128]{1,0:T(8,128)(2,1)S(1)}, bf16[512,128]{1,0:T(8,128)(2,1)}, u32[]{:S(2)}) copy-start(bf16[512,128]{1,0:T(8,128)(2,1)} %value.3) | copy-start | bytes 393220
  29.3 20.8 %copy-start.3 = (bf16[512,128]{1,0:T(8,128)(2,1)S(1)}, bf16[512,128]{1,0:T(8,128)(2,1)}, u32[]{:S(2)}) copy-start(bf16[512,128]{1,0:T(8,128)(2,1)} %grad.3) | copy-start | bytes 393220
